TPU v7x, 512 devices: a whole 4x8x8 slice. The times are simulated.
512 devices in a mesh: row: 16 (over x, y_lo), col: 32 (over y_hi, z, core).
Axes of the slice: x: 4, y: 8 (y_hi: 2, y_lo: 4; y = y_hi * 4 + y_lo), z: 8, core: 2. Of those that a mesh axis runs over, the one named last changes fastest.
Arguments:
- row_ids: int32 [128], P('row'), may hold values from -1 to 127, as said below
- a_tiles: bfloat16 [8192, 4096], P('row', 'col'), may hold values from -6 to 6
- a_mask: int32 [128, 64], P('row', 'col'), may hold values 0 or 1
- b_tiles: bfloat16 [4096, 24576], P('row', 'col'), may hold values from -0.1875 to 0.1875
- b_mask: int32 [64, 384], P('row', 'col'), may hold values 0 or 1
- c_keep: int32 [128, 384], P(None, 'col'), may hold values 0 or 1
Outputs:
- product_out: bfloat16 [8192, 24576], P('row', 'col')
Inputs may be any that keep to these rules, and one draw needn't show every extreme that they name: `row_ids`: within a group of 8 slots the live ids come first and -1 fills the rest; live ids are distinct over all slots; every group has at least half of its slots live and some group has all 8 live.
All inputs are finite; a program needn't handle non-finite values. No bound on the sum of `a_mask` or of `b_mask` or of `c_keep` on one device may be relied on, other than what follows from the above.
Results may differ from a plain program's by a relative error of at most 0.001.
Values may be sent and summed in bfloat16 or wider, within the bound.
A program may use at most 64 MiB of HBM per device.

v0:
```python
import jax
import jax.numpy as jnp
from jax import lax
from jax.sharding import PartitionSpec as P

TILE = 64


def passed_along(block, axis, distance):
    devices = range(lax.axis_size(axis))
    route = [((i - distance) % len(devices), i) for i in devices]
    return lax.ppermute(block, axis, route)


def per_device(row_ids, a_tiles, a_mask, b_tiles, b_mask, c_keep):
    col_count = lax.axis_size("col")
    row_count = lax.axis_size("row")
    ratio_cols = col_count // row_count
    tile_edge = TILE
    slot_count = a_mask.shape[0]
    panel_blocks = a_mask.shape[1]
    column_blocks = b_mask.shape[1]
    panel_rows = panel_blocks * tile_edge
    a_eff = (
        a_tiles.reshape(slot_count, tile_edge, panel_blocks, tile_edge)
        * a_mask.astype(jnp.bfloat16)[:, None, :, None]
    )
    a_eff = a_eff.reshape(a_tiles.shape)
    b_eff = (
        b_tiles.reshape(b_mask.shape[0], tile_edge, column_blocks, tile_edge)
        * b_mask.astype(jnp.bfloat16)[:, None, :, None]
    )
    b_eff = b_eff.reshape(b_tiles.shape)
    running = jnp.zeros((a_tiles.shape[0], b_tiles.shape[1]), jnp.float32)

    def outer_step(group_step, carry):
        total, a_current, b_current = carry
        for inner_step in range(ratio_cols):
            local_panel = ratio_cols - 1 - inner_step
            b_rows = b_current[local_panel * panel_rows : (local_panel + 1) * panel_rows]
            total = total + jnp.dot(a_current, b_rows, preferred_element_type=jnp.float32)
            a_current = passed_along(a_current, "col", 1)
        b_current = passed_along(b_current, "row", 1)
        return (total, a_current, b_current)

    running, a_last, b_last = lax.fori_loop(0, row_count, outer_step, (running, a_eff, b_eff))
    onehot = (row_ids[:, None] == jnp.arange(c_keep.shape[0], dtype=jnp.int32)[None, :]).astype(
        jnp.float32
    )
    keep = jnp.dot(onehot, c_keep.astype(jnp.float32))
    masked = (
        running.reshape(slot_count, tile_edge, column_blocks, tile_edge) * keep[:, None, :, None]
    )
    return masked.reshape(running.shape).astype(jnp.bfloat16)


def solution(mesh):
    placed = (
        P("row"),
        P("row", "col"),
        P("row", "col"),
        P("row", "col"),
        P("row", "col"),
        P(None, "col"),
    )
    return jax.shard_map(
        per_device, mesh=mesh, in_specs=placed, out_specs=P("row", "col"), check_vma=False
    )
```

profile of v0, /device:TPU:8, one launch (start us, length us, event | category | flops | bytes accessed | tf_op | source)
XLA Modules:
  0.0 450.8 jit_solution(16547820729961444386)
XLA Ops:
  7.4 436.5 %while.15 = (s32[]{:T(128)}, f32[512,768]{1,0:T(8,128)S(1)}, bf16[512,128]{1,0:T(8,128)(2,1)}, bf16[256,768]{1,0:T(8,128)(2,1)}, s32[]{:T(128)}, /*index=5*/s32[]{:T(128)}) while((s32[]{:T(128)}, f32[512,768]{1,0:T(8,128)S(1)}, bf16[512,128]{1,0:T(8,128)(2,1)}, bf16[256,768]{1,0:T(8,128)(2,1)}, s32[]{:T(128)}, ...), condition=%wide.region_1.0_spmd.clone, body=%wide.region_0.0_spmd.clone.sunk | while | flops 202506240 | bytes 10354887 | solution.py:46
  10.3 3.5 collective-permute-start.2
  15.0 10.4 %collective-permute-done = bf16[512,128]{1,0:T(8,128)(2,1)} collective-permute-done((bf16[512,128]{1,0:T(8,128)(2,1)}, bf16[512,128]{1,0:T(8,128)(2,1)}, u32[]{:S(2)}, u32[]{:S(2)}) %collective-permute-start) | collective-permute-done | bytes 131104 | tf_op jit(solution)/shard_map/while/body/eval_jaxpr/ppermute | solution.py:12
  25.4 1.9 collective-permute-start.1
  28.6 12.7 %collective-permute-done.1 = bf16[512,128]{1,0:T(8,128)(2,1)} collective-permute-done((bf16[512,128]{1,0:T(8,128)(2,1)}, bf16[512,128]{1,0:T(8,128)(2,1)}, u32[]{:S(2)}, u32[]{:S(2)}) %collective-permute-start.1) | collective-permute-done | bytes 131104 | tf_op jit(solution)/shard_map/while/body/eval_jaxpr/ppermute | solution.py:12
  41.4 1.9 collective-permute-start
  47.5 10.3 %collective-permute-done = bf16[512,128]{1,0:T(8,128)(2,1)} collective-permute-done((bf16[512,128]{1,0:T(8,128)(2,1)}, bf16[512,128]{1,0:T(8,128)(2,1)}, u32[]{:S(2)}, u32[]{:S(2)}) %collective-permute-start) | collective-permute-done | bytes 131104 | tf_op jit(solution)/shard_map/while/body/eval_jaxpr/ppermute | solution.py:12
  57.7 1.9 collective-permute-start.1
  60.9 9.4 %collective-permute-done.1 = bf16[512,128]{1,0:T(8,128)(2,1)} collective-permute-done((bf16[512,128]{1,0:T(8,128)(2,1)}, bf16[512,128]{1,0:T(8,128)(2,1)}, u32[]{:S(2)}, u32[]{:S(2)}) %collective-permute-start.1) | collective-permute-done | bytes 131104 | tf_op jit(solution)/shard_map/while/body/eval_jaxpr/ppermute | solution.py:12
  70.4 1.9 collective-permute-start
  76.4 8.6 %collective-permute-done = bf16[512,128]{1,0:T(8,128)(2,1)} collective-permute-done((bf16[512,128]{1,0:T(8,128)(2,1)}, bf16[512,128]{1,0:T(8,128)(2,1)}, u32[]{:S(2)}, u32[]{:S(2)}) %collective-permute-start) | collective-permute-done | bytes 131104 | tf_op jit(solution)/shard_map/while/body/eval_jaxpr/ppermute | solution.py:12
  85.0 1.9 collective-permute-start.1
  88.2 9.4 %collective-permute-done.1 = bf16[512,128]{1,0:T(8,128)(2,1)} collective-permute-done((bf16[512,128]{1,0:T(8,128)(2,1)}, bf16[512,128]{1,0:T(8,128)(2,1)}, u32[]{:S(2)}, u32[]{:S(2)}) %collective-permute-start.1) | collective-permute-done | bytes 131104 | tf_op jit(solution)/shard_map/while/body/eval_jaxpr/ppermute | solution.py:12
  97.6 1.9 collective-permute-start
  103.7 7.9 %collective-permute-done = bf16[512,128]{1,0:T(8,128)(2,1)} collective-permute-done((bf16[512,128]{1,0:T(8,128)(2,1)}, bf16[512,128]{1,0:T(8,128)(2,1)}, u32[]{:S(2)}, u32[]{:S(2)}) %collective-permute-start) | collective-permute-done | bytes 131104 | tf_op jit(solution)/shard_map/while/body/eval_jaxpr/ppermute | solution.py:12
  111.6 1.9 collective-permute-start.1
  114.8 9.4 %collective-permute-done.1 = bf16[512,128]{1,0:T(8,128)(2,1)} collective-permute-done((bf16[512,128]{1,0:T(8,128)(2,1)}, bf16[512,128]{1,0:T(8,128)(2,1)}, u32[]{:S(2)}, u32[]{:S(2)}) %collective-permute-start.1) | collective-permute-done | bytes 131104 | tf_op jit(solution)/shard_map/while/body/eval_jaxpr/ppermute | solution.py:12
  124.2 1.9 collective-permute-start
  130.3 7.3 %collective-permute-done = bf16[512,128]{1,0:T(8,128)(2,1)} collective-permute-done((bf16[512,128]{1,0:T(8,128)(2,1)}, bf16[512,128]{1,0:T(8,128)(2,1)}, u32[]{:S(2)}, u32[]{:S(2)}) %collective-permute-start) | collective-permute-done | bytes 131104 | tf_op jit(solution)/shard_map/while/body/eval_jaxpr/ppermute | solution.py:12
  137.6 1.9 collective-permute-start.1
  140.8 9.4 %collective-permute-done.1 = bf16[512,128]{1,0:T(8,128)(2,1)} collective-permute-done((bf16[512,128]{1,0:T(8,128)(2,1)}, bf16[512,128]{1,0:T(8,128)(2,1)}, u32[]{:S(2)}, u32[]{:S(2)}) %collective-permute-start.1) | collective-permute-done | bytes 131104 | tf_op jit(solution)/shard_map/while/body/eval_jaxpr/ppermute | solution.py:12
  150.3 1.9 collective-permute-start
  156.3 8.4 %collective-permute-done = bf16[512,128]{1,0:T(8,128)(2,1)} collective-permute-done((bf16[512,128]{1,0:T(8,128)(2,1)}, bf16[512,128]{1,0:T(8,128)(2,1)}, u32[]{:S(2)}, u32[]{:S(2)}) %collective-permute-start) | collective-permute-done | bytes 131104 | tf_op jit(solution)/shard_map/while/body/eval_jaxpr/ppermute | solution.py:12
  164.8 1.9 collective-permute-start.1
  168.0 9.4 %collective-permute-done.1 = bf16[512,128]{1,0:T(8,128)(2,1)} collective-permute-done((bf16[512,128]{1,0:T(8,128)(2,1)}, bf16[512,128]{1,0:T(8,128)(2,1)}, u32[]{:S(2)}, u32[]{:S(2)}) %collective-permute-start.1) | collective-permute-done | bytes 131104 | tf_op jit(solution)/shard_map/while/body/eval_jaxpr/ppermute | solution.py:12
  177.4 1.9 collective-permute-start
  183.5 7.6 %collective-permute-done = bf16[512,128]{1,0:T(8,128)(2,1)} collective-permute-done((bf16[512,128]{1,0:T(8,128)(2,1)}, bf16[512,128]{1,0:T(8,128)(2,1)}, u32[]{:S(2)}, u32[]{:S(2)}) %collective-permute-start) | collective-permute-done | bytes 131104 | tf_op jit(solution)/shard_map/while/body/eval_jaxpr/ppermute | solution.py:12
  191.0 1.9 collective-permute-start.1
  194.2 9.4 %collective-permute-done.1 = bf16[512,128]{1,0:T(8,128)(2,1)} collective-permute-done((bf16[512,128]{1,0:T(8,128)(2,1)}, bf16[512,128]{1,0:T(8,128)(2,1)}, u32[]{:S(2)}, u32[]{:S(2)}) %collective-permute-start.1) | collective-permute-done | bytes 131104 | tf_op jit(solution)/shard_map/while/body/eval_jaxpr/ppermute | solution.py:12
  203.6 1.9 collective-permute-start
  209.7 8.0 %collective-permute-done = bf16[512,128]{1,0:T(8,128)(2,1)} collective-permute-done((bf16[512,128]{1,0:T(8,128)(2,1)}, bf16[512,128]{1,0:T(8,128)(2,1)}, u32[]{:S(2)}, u32[]{:S(2)}) %collective-permute-start) | collective-permute-done | bytes 131104 | tf_op jit(solution)/shard_map/while/body/eval_jaxpr/ppermute | solution.py:12
  217.7 1.9 collective-permute-start.1
  220.9 9.4 %collective-permute-done.1 = bf16[512,128]{1,0:T(8,128)(2,1)} collective-permute-done((bf16[512,128]{1,0:T(8,128)(2,1)}, bf16[512,128]{1,0:T(8,128)(2,1)}, u32[]{:S(2)}, u32[]{:S(2)}) %collective-permute-start.1) | collective-permute-done | bytes 131104 | tf_op jit(solution)/shard_map/while/body/eval_jaxpr/ppermute | solution.py:12
  230.3 1.9 collective-permute-start
  236.4 8.0 %collective-permute-done = bf16[512,128]{1,0:T(8,128)(2,1)} collective-permute-done((bf16[512,128]{1,0:T(8,128)(2,1)}, bf16[512,128]{1,0:T(8,128)(2,1)}, u32[]{:S(2)}, u32[]{:S(2)}) %collective-permute-start) | collective-permute-done | bytes 131104 | tf_op jit(solution)/shard_map/while/body/eval_jaxpr/ppermute | solution.py:12
  244.4 1.9 collective-permute-start.1
  247.6 9.4 %collective-permute-done.1 = bf16[512,128]{1,0:T(8,128)(2,1)} collective-permute-done((bf16[512,128]{1,0:T(8,128)(2,1)}, bf16[512,128]{1,0:T(8,128)(2,1)}, u32[]{:S(2)}, u32[]{:S(2)}) %collective-permute-start.1) | collective-permute-done | bytes 131104 | tf_op jit(solution)/shard_map/while/body/eval_jaxpr/ppermute | solution.py:12
  257.0 1.9 collective-permute-start
  263.1 8.0 %collective-permute-done = bf16[512,128]{1,0:T(8,128)(2,1)} collective-permute-done((bf16[512,128]{1,0:T(8,128)(2,1)}, bf16[512,128]{1,0:T(8,128)(2,1)}, u32[]{:S(2)}, u32[]{:S(2)}) %collective-permute-start) | collective-permute-done | bytes 131104 | tf_op jit(solution)/shard_map/while/body/eval_jaxpr/ppermute | solution.py:12
  271.1 1.9 collective-permute-start.1
  274.3 9.4 %collective-permute-done.1 = bf16[512,128]{1,0:T(8,128)(2,1)} collective-permute-done((bf16[512,128]{1,0:T(8,128)(2,1)}, bf16[512,128]{1,0:T(8,128)(2,1)}, u32[]{:S(2)}, u32[]{:S(2)}) %collective-permute-start.1) | collective-permute-done | bytes 131104 | tf_op jit(solution)/shard_map/while/body/eval_jaxpr/ppermute | solution.py:12
  283.7 1.9 collective-permute-start
  289.8 8.0 %collective-permute-done = bf16[512,128]{1,0:T(8,128)(2,1)} collective-permute-done((bf16[512,128]{1,0:T(8,128)(2,1)}, bf16[512,128]{1,0:T(8,128)(2,1)}, u32[]{:S(2)}, u32[]{:S(2)}) %collective-permute-start) | collective-permute-done | bytes 131104 | tf_op jit(solution)/shard_map/while/body/eval_jaxpr/ppermute | solution.py:12
  297.8 1.9 collective-permute-start.1
  301.0 9.4 %collective-permute-done.1 = bf16[512,128]{1,0:T(8,128)(2,1)} collective-permute-done((bf16[512,128]{1,0:T(8,128)(2,1)}, bf16[512,128]{1,0:T(8,128)(2,1)}, u32[]{:S(2)}, u32[]{:S(2)}) %collective-permute-start.1) | collective-permute-done | bytes 131104 | tf_op jit(solution)/shard_map/while/body/eval_jaxpr/ppermute | solution.py:12
  310.4 1.9 collective-permute-start
  316.5 8.0 %collective-permute-done = bf16[512,128]{1,0:T(8,128)(2,1)} collective-permute-done((bf16[512,128]{1,0:T(8,128)(2,1)}, bf16[512,128]{1,0:T(8,128)(2,1)}, u32[]{:S(2)}, u32[]{:S(2)}) %collective-permute-start) | collective-permute-done | bytes 131104 | tf_op jit(solution)/shard_map/while/body/eval_jaxpr/ppermute | solution.py:12
  324.5 1.9 collective-permute-start.1
  327.7 9.4 %collective-permute-done.1 = bf16[512,128]{1,0:T(8,128)(2,1)} collective-permute-done((bf16[512,128]{1,0:T(8,128)(2,1)}, bf16[512,128]{1,0:T(8,128)(2,1)}, u32[]{:S(2)}, u32[]{:S(2)}) %collective-permute-start.1) | collective-permute-done | bytes 131104 | tf_op jit(solution)/shard_map/while/body/eval_jaxpr/ppermute | solution.py:12
  337.1 1.9 collective-permute-start
  343.2 8.0 %collective-permute-done = bf16[512,128]{1,0:T(8,128)(2,1)} collective-permute-done((bf16[512,128]{1,0:T(8,128)(2,1)}, bf16[512,128]{1,0:T(8,128)(2,1)}, u32[]{:S(2)}, u32[]{:S(2)}) %collective-permute-start) | collective-permute-done | bytes 131104 | tf_op jit(solution)/shard_map/while/body/eval_jaxpr/ppermute | solution.py:12
  351.2 1.9 collective-permute-start.1
  354.4 9.4 %collective-permute-done.1 = bf16[512,128]{1,0:T(8,128)(2,1)} collective-permute-done((bf16[512,128]{1,0:T(8,128)(2,1)}, bf16[512,128]{1,0:T(8,128)(2,1)}, u32[]{:S(2)}, u32[]{:S(2)}) %collective-permute-start.1) | collective-permute-done | bytes 131104 | tf_op jit(solution)/shard_map/while/body/eval_jaxpr/ppermute | solution.py:12
  363.8 1.9 collective-permute-start
  369.9 8.0 %collective-permute-done = bf16[512,128]{1,0:T(8,128)(2,1)} collective-permute-done((bf16[512,128]{1,0:T(8,128)(2,1)}, bf16[512,128]{1,0:T(8,128)(2,1)}, u32[]{:S(2)}, u32[]{:S(2)}) %collective-permute-start) | collective-permute-done | bytes 131104 | tf_op jit(solution)/shard_map/while/body/eval_jaxpr/ppermute | solution.py:12
  377.9 1.9 collective-permute-start.1
  381.1 9.4 %collective-permute-done.1 = bf16[512,128]{1,0:T(8,128)(2,1)} collective-permute-done((bf16[512,128]{1,0:T(8,128)(2,1)}, bf16[512,128]{1,0:T(8,128)(2,1)}, u32[]{:S(2)}, u32[]{:S(2)}) %collective-permute-start.1) | collective-permute-done | bytes 131104 | tf_op jit(solution)/shard_map/while/body/eval_jaxpr/ppermute | solution.py:12
  390.5 1.9 collective-permute-start
  396.6 8.0 %collective-permute-done = bf16[512,128]{1,0:T(8,128)(2,1)} collective-permute-done((bf16[512,128]{1,0:T(8,128)(2,1)}, bf16[512,128]{1,0:T(8,128)(2,1)}, u32[]{:S(2)}, u32[]{:S(2)}) %collective-permute-start) | collective-permute-done | bytes 131104 | tf_op jit(solution)/shard_map/while/body/eval_jaxpr/ppermute | solution.py:12
  407.8 9.4 %collective-permute-done.1 = bf16[512,128]{1,0:T(8,128)(2,1)} collective-permute-done((bf16[512,128]{1,0:T(8,128)(2,1)}, bf16[512,128]{1,0:T(8,128)(2,1)}, u32[]{:S(2)}, u32[]{:S(2)}) %collective-permute-start.1) | collective-permute-done | bytes 131104 | tf_op jit(solution)/shard_map/while/body/eval_jaxpr/ppermute | solution.py:12
  417.2 1.9 collective-permute-start
  423.3 8.0 %collective-permute-done = bf16[512,128]{1,0:T(8,128)(2,1)} collective-permute-done((bf16[512,128]{1,0:T(8,128)(2,1)}, bf16[512,128]{1,0:T(8,128)(2,1)}, u32[]{:S(2)}, u32[]{:S(2)}) %collective-permute-start) | collective-permute-done | bytes 131104 | tf_op jit(solution)/shard_map/while/body/eval_jaxpr/ppermute | solution.py:12
  434.5 9.4 %collective-permute-done.1 = bf16[512,128]{1,0:T(8,128)(2,1)} collective-permute-done((bf16[512,128]{1,0:T(8,128)(2,1)}, bf16[512,128]{1,0:T(8,128)(2,1)}, u32[]{:S(2)}, u32[]{:S(2)}) %collective-permute-start.1) | collective-permute-done | bytes 131104 | tf_op jit(solution)/shard_map/while/body/eval_jaxpr/ppermute | solution.py:12
  447.5 2.1 multiply_convert_fusion
  (100 shorter events, 102.8 us)
Async XLA Ops:
  7.4 18.1 %collective-permute-start = (bf16[512,128]{1,0:T(8,128)(2,1)}, bf16[512,128]{1,0:T(8,128)(2,1)}, u32[]{:S(2)}, u32[]{:S(2)}) collective-permute-start(bf16[512,128]{1,0:T(8,128)(2,1)} %get-tuple-element.88), channel_id=1, source_target_pairs={{31,0},{0,1},{1,2},{2,3},{3,4},{4,5},{5,6},{6,7},{7,8},{8,9},{9,10... | collective-permute-start | bytes 393224 | tf_op jit(solution)/shard_map/while/body/eval_jaxpr/ppermute | solution.py:12
  10.3 31.1 %collective-permute-start.2 = (bf16[256,768]{1,0:T(8,128)(2,1)S(1)}, bf16[256,768]{1,0:T(8,128)(2,1)}, u32[]{:S(2)}, u32[]{:S(2)}) collective-permute-start(bf16[256,768]{1,0:T(8,128)(2,1)S(1)} %copy.23), channel_id=1, source_target_pairs={{480,0},{0,32},{32,64},{64,96},{96,128},{128,160},{160,192},{192,2... | collective-permute-start | bytes 1179656 | tf_op jit(solution)/shard_map/while/body/eval_jaxpr/ppermute | solution.py:12
  25.4 15.9 %collective-permute-start.1 = (bf16[512,128]{1,0:T(8,128)(2,1)}, bf16[512,128]{1,0:T(8,128)(2,1)}, u32[]{:S(2)}, u32[]{:S(2)}) collective-permute-start(bf16[512,128]{1,0:T(8,128)(2,1)} %collective-permute-done), channel_id=1, source_target_pairs={{31,0},{0,1},{1,2},{2,3},{3,4},{4,5},{5,6},{6,7},{7,8},{8,9},{9,10... | collective-permute-start | bytes 393224 | tf_op jit(solution)/shard_map/while/body/eval_jaxpr/ppermute | solution.py:12
  41.4 16.3 %collective-permute-start = (bf16[512,128]{1,0:T(8,128)(2,1)}, bf16[512,128]{1,0:T(8,128)(2,1)}, u32[]{:S(2)}, u32[]{:S(2)}) collective-permute-start(bf16[512,128]{1,0:T(8,128)(2,1)} %get-tuple-element.88), channel_id=1, source_target_pairs={{31,0},{0,1},{1,2},{2,3},{3,4},{4,5},{5,6},{6,7},{7,8},{8,9},{9,10... | collective-permute-start | bytes 393224 | tf_op jit(solution)/shard_map/while/body/eval_jaxpr/ppermute | solution.py:12
  44.3 26.0 %collective-permute-start.2 = (bf16[256,768]{1,0:T(8,128)(2,1)S(1)}, bf16[256,768]{1,0:T(8,128)(2,1)}, u32[]{:S(2)}, u32[]{:S(2)}) collective-permute-start(bf16[256,768]{1,0:T(8,128)(2,1)S(1)} %copy.23), channel_id=1, source_target_pairs={{480,0},{0,32},{32,64},{64,96},{96,128},{128,160},{160,192},{192,2... | collective-permute-start | bytes 1179656 | tf_op jit(solution)/shard_map/while/body/eval_jaxpr/ppermute | solution.py:12
  57.7 12.6 %collective-permute-start.1 = (bf16[512,128]{1,0:T(8,128)(2,1)}, bf16[512,128]{1,0:T(8,128)(2,1)}, u32[]{:S(2)}, u32[]{:S(2)}) collective-permute-start(bf16[512,128]{1,0:T(8,128)(2,1)} %collective-permute-done), channel_id=1, source_target_pairs={{31,0},{0,1},{1,2},{2,3},{3,4},{4,5},{5,6},{6,7},{7,8},{8,9},{9,10... | collective-permute-start | bytes 393224 | tf_op jit(solution)/shard_map/while/body/eval_jaxpr/ppermute | solution.py:12
  70.4 14.7 %collective-permute-start = (bf16[512,128]{1,0:T(8,128)(2,1)}, bf16[512,128]{1,0:T(8,128)(2,1)}, u32[]{:S(2)}, u32[]{:S(2)}) collective-permute-start(bf16[512,128]{1,0:T(8,128)(2,1)} %get-tuple-element.88), channel_id=1, source_target_pairs={{31,0},{0,1},{1,2},{2,3},{3,4},{4,5},{5,6},{6,7},{7,8},{8,9},{9,10... | collective-permute-start | bytes 393224 | tf_op jit(solution)/shard_map/while/body/eval_jaxpr/ppermute | solution.py:12
  73.3 24.4 %collective-permute-start.2 = (bf16[256,768]{1,0:T(8,128)(2,1)S(1)}, bf16[256,768]{1,0:T(8,128)(2,1)}, u32[]{:S(2)}, u32[]{:S(2)}) collective-permute-start(bf16[256,768]{1,0:T(8,128)(2,1)S(1)} %copy.23), channel_id=1, source_target_pairs={{480,0},{0,32},{32,64},{64,96},{96,128},{128,160},{160,192},{192,2... | collective-permute-start | bytes 1179656 | tf_op jit(solution)/shard_map/while/body/eval_jaxpr/ppermute | solution.py:12
  85.0 12.6 %collective-permute-start.1 = (bf16[512,128]{1,0:T(8,128)(2,1)}, bf16[512,128]{1,0:T(8,128)(2,1)}, u32[]{:S(2)}, u32[]{:S(2)}) collective-permute-start(bf16[512,128]{1,0:T(8,128)(2,1)} %collective-permute-done), channel_id=1, source_target_pairs={{31,0},{0,1},{1,2},{2,3},{3,4},{4,5},{5,6},{6,7},{7,8},{8,9},{9,10... | collective-permute-start | bytes 393224 | tf_op jit(solution)/shard_map/while/body/eval_jaxpr/ppermute | solution.py:12
  97.6 14.0 %collective-permute-start = (bf16[512,128]{1,0:T(8,128)(2,1)}, bf16[512,128]{1,0:T(8,128)(2,1)}, u32[]{:S(2)}, u32[]{:S(2)}) collective-permute-start(bf16[512,128]{1,0:T(8,128)(2,1)} %get-tuple-element.88), channel_id=1, source_target_pairs={{31,0},{0,1},{1,2},{2,3},{3,4},{4,5},{5,6},{6,7},{7,8},{8,9},{9,10... | collective-permute-start | bytes 393224 | tf_op jit(solution)/shard_map/while/body/eval_jaxpr/ppermute | solution.py:12
  100.5 23.7 %collective-permute-start.2 = (bf16[256,768]{1,0:T(8,128)(2,1)S(1)}, bf16[256,768]{1,0:T(8,128)(2,1)}, u32[]{:S(2)}, u32[]{:S(2)}) collective-permute-start(bf16[256,768]{1,0:T(8,128)(2,1)S(1)} %copy.23), channel_id=1, source_target_pairs={{480,0},{0,32},{32,64},{64,96},{96,128},{128,160},{160,192},{192,2... | collective-permute-start | bytes 1179656 | tf_op jit(solution)/shard_map/while/body/eval_jaxpr/ppermute | solution.py:12
  111.6 12.6 %collective-permute-start.1 = (bf16[512,128]{1,0:T(8,128)(2,1)}, bf16[512,128]{1,0:T(8,128)(2,1)}, u32[]{:S(2)}, u32[]{:S(2)}) collective-permute-start(bf16[512,128]{1,0:T(8,128)(2,1)} %collective-permute-done), channel_id=1, source_target_pairs={{31,0},{0,1},{1,2},{2,3},{3,4},{4,5},{5,6},{6,7},{7,8},{8,9},{9,10... | collective-permute-start | bytes 393224 | tf_op jit(solution)/shard_map/while/body/eval_jaxpr/ppermute | solution.py:12
  124.2 13.4 %collective-permute-start = (bf16[512,128]{1,0:T(8,128)(2,1)}, bf16[512,128]{1,0:T(8,128)(2,1)}, u32[]{:S(2)}, u32[]{:S(2)}) collective-permute-start(bf16[512,128]{1,0:T(8,128)(2,1)} %get-tuple-element.88), channel_id=1, source_target_pairs={{31,0},{0,1},{1,2},{2,3},{3,4},{4,5},{5,6},{6,7},{7,8},{8,9},{9,10... | collective-permute-start | bytes 393224 | tf_op jit(solution)/shard_map/while/body/eval_jaxpr/ppermute | solution.py:12
  127.1 23.1 %collective-permute-start.2 = (bf16[256,768]{1,0:T(8,128)(2,1)S(1)}, bf16[256,768]{1,0:T(8,128)(2,1)}, u32[]{:S(2)}, u32[]{:S(2)}) collective-permute-start(bf16[256,768]{1,0:T(8,128)(2,1)S(1)} %copy.23), channel_id=1, source_target_pairs={{480,0},{0,32},{32,64},{64,96},{96,128},{128,160},{160,192},{192,2... | collective-permute-start | bytes 1179656 | tf_op jit(solution)/shard_map/while/body/eval_jaxpr/ppermute | solution.py:12
  137.6 12.6 %collective-permute-start.1 = (bf16[512,128]{1,0:T(8,128)(2,1)}, bf16[512,128]{1,0:T(8,128)(2,1)}, u32[]{:S(2)}, u32[]{:S(2)}) collective-permute-start(bf16[512,128]{1,0:T(8,128)(2,1)} %collective-permute-done), channel_id=1, source_target_pairs={{31,0},{0,1},{1,2},{2,3},{3,4},{4,5},{5,6},{6,7},{7,8},{8,9},{9,10... | collective-permute-start | bytes 393224 | tf_op jit(solution)/shard_map/while/body/eval_jaxpr/ppermute | solution.py:12
  150.3 14.5 %collective-permute-start = (bf16[512,128]{1,0:T(8,128)(2,1)}, bf16[512,128]{1,0:T(8,128)(2,1)}, u32[]{:S(2)}, u32[]{:S(2)}) collective-permute-start(bf16[512,128]{1,0:T(8,128)(2,1)} %get-tuple-element.88), channel_id=1, source_target_pairs={{31,0},{0,1},{1,2},{2,3},{3,4},{4,5},{5,6},{6,7},{7,8},{8,9},{9,10... | collective-permute-start | bytes 393224 | tf_op jit(solution)/shard_map/while/body/eval_jaxpr/ppermute | solution.py:12
  153.2 24.2 %collective-permute-start.2 = (bf16[256,768]{1,0:T(8,128)(2,1)S(1)}, bf16[256,768]{1,0:T(8,128)(2,1)}, u32[]{:S(2)}, u32[]{:S(2)}) collective-permute-start(bf16[256,768]{1,0:T(8,128)(2,1)S(1)} %copy.23), channel_id=1, source_target_pairs={{480,0},{0,32},{32,64},{64,96},{96,128},{128,160},{160,192},{192,2... | collective-permute-start | bytes 1179656 | tf_op jit(solution)/shard_map/while/body/eval_jaxpr/ppermute | solution.py:12
  164.8 12.6 %collective-permute-start.1 = (bf16[512,128]{1,0:T(8,128)(2,1)}, bf16[512,128]{1,0:T(8,128)(2,1)}, u32[]{:S(2)}, u32[]{:S(2)}) collective-permute-start(bf16[512,128]{1,0:T(8,128)(2,1)} %collective-permute-done), channel_id=1, source_target_pairs={{31,0},{0,1},{1,2},{2,3},{3,4},{4,5},{5,6},{6,7},{7,8},{8,9},{9,10... | collective-permute-start | bytes 393224 | tf_op jit(solution)/shard_map/while/body/eval_jaxpr/ppermute | solution.py:12
  177.4 13.7 %collective-permute-start = (bf16[512,128]{1,0:T(8,128)(2,1)}, bf16[512,128]{1,0:T(8,128)(2,1)}, u32[]{:S(2)}, u32[]{:S(2)}) collective-permute-start(bf16[512,128]{1,0:T(8,128)(2,1)} %get-tuple-element.88), channel_id=1, source_target_pairs={{31,0},{0,1},{1,2},{2,3},{3,4},{4,5},{5,6},{6,7},{7,8},{8,9},{9,10... | collective-permute-start | bytes 393224 | tf_op jit(solution)/shard_map/while/body/eval_jaxpr/ppermute | solution.py:12
  180.3 23.3 %collective-permute-start.2 = (bf16[256,768]{1,0:T(8,128)(2,1)S(1)}, bf16[256,768]{1,0:T(8,128)(2,1)}, u32[]{:S(2)}, u32[]{:S(2)}) collective-permute-start(bf16[256,768]{1,0:T(8,128)(2,1)S(1)} %copy.23), channel_id=1, source_target_pairs={{480,0},{0,32},{32,64},{64,96},{96,128},{128,160},{160,192},{192,2... | collective-permute-start | bytes 1179656 | tf_op jit(solution)/shard_map/while/body/eval_jaxpr/ppermute | solution.py:12
  191.0 12.6 %collective-permute-start.1 = (bf16[512,128]{1,0:T(8,128)(2,1)}, bf16[512,128]{1,0:T(8,128)(2,1)}, u32[]{:S(2)}, u32[]{:S(2)}) collective-permute-start(bf16[512,128]{1,0:T(8,128)(2,1)} %collective-permute-done), channel_id=1, source_target_pairs={{31,0},{0,1},{1,2},{2,3},{3,4},{4,5},{5,6},{6,7},{7,8},{8,9},{9,10... | collective-permute-start | bytes 393224 | tf_op jit(solution)/shard_map/while/body/eval_jaxpr/ppermute | solution.py:12
  203.6 14.1 %collective-permute-start = (bf16[512,128]{1,0:T(8,128)(2,1)}, bf16[512,128]{1,0:T(8,128)(2,1)}, u32[]{:S(2)}, u32[]{:S(2)}) collective-permute-start(bf16[512,128]{1,0:T(8,128)(2,1)} %get-tuple-element.88), channel_id=1, source_target_pairs={{31,0},{0,1},{1,2},{2,3},{3,4},{4,5},{5,6},{6,7},{7,8},{8,9},{9,10... | collective-permute-start | bytes 393224 | tf_op jit(solution)/shard_map/while/body/eval_jaxpr/ppermute | solution.py:12
  206.6 23.8 %collective-permute-start.2 = (bf16[256,768]{1,0:T(8,128)(2,1)S(1)}, bf16[256,768]{1,0:T(8,128)(2,1)}, u32[]{:S(2)}, u32[]{:S(2)}) collective-permute-start(bf16[256,768]{1,0:T(8,128)(2,1)S(1)} %copy.23), channel_id=1, source_target_pairs={{480,0},{0,32},{32,64},{64,96},{96,128},{128,160},{160,192},{192,2... | collective-permute-start | bytes 1179656 | tf_op jit(solution)/shard_map/while/body/eval_jaxpr/ppermute | solution.py:12
  217.7 12.6 %collective-permute-start.1 = (bf16[512,128]{1,0:T(8,128)(2,1)}, bf16[512,128]{1,0:T(8,128)(2,1)}, u32[]{:S(2)}, u32[]{:S(2)}) collective-permute-start(bf16[512,128]{1,0:T(8,128)(2,1)} %collective-permute-done), channel_id=1, source_target_pairs={{31,0},{0,1},{1,2},{2,3},{3,4},{4,5},{5,6},{6,7},{7,8},{8,9},{9,10... | collective-permute-start | bytes 393224 | tf_op jit(solution)/shard_map/while/body/eval_jaxpr/ppermute | solution.py:12
  230.3 14.1 %collective-permute-start = (bf16[512,128]{1,0:T(8,128)(2,1)}, bf16[512,128]{1,0:T(8,128)(2,1)}, u32[]{:S(2)}, u32[]{:S(2)}) collective-permute-start(bf16[512,128]{1,0:T(8,128)(2,1)} %get-tuple-element.88), channel_id=1, source_target_pairs={{31,0},{0,1},{1,2},{2,3},{3,4},{4,5},{5,6},{6,7},{7,8},{8,9},{9,10... | collective-permute-start | bytes 393224 | tf_op jit(solution)/shard_map/while/body/eval_jaxpr/ppermute | solution.py:12
  233.2 23.8 %collective-permute-start.2 = (bf16[256,768]{1,0:T(8,128)(2,1)S(1)}, bf16[256,768]{1,0:T(8,128)(2,1)}, u32[]{:S(2)}, u32[]{:S(2)}) collective-permute-start(bf16[256,768]{1,0:T(8,128)(2,1)S(1)} %copy.23), channel_id=1, source_target_pairs={{480,0},{0,32},{32,64},{64,96},{96,128},{128,160},{160,192},{192,2... | collective-permute-start | bytes 1179656 | tf_op jit(solution)/shard_map/while/body/eval_jaxpr/ppermute | solution.py:12
  244.4 12.6 %collective-permute-start.1 = (bf16[512,128]{1,0:T(8,128)(2,1)}, bf16[512,128]{1,0:T(8,128)(2,1)}, u32[]{:S(2)}, u32[]{:S(2)}) collective-permute-start(bf16[512,128]{1,0:T(8,128)(2,1)} %collective-permute-done), channel_id=1, source_target_pairs={{31,0},{0,1},{1,2},{2,3},{3,4},{4,5},{5,6},{6,7},{7,8},{8,9},{9,10... | collective-permute-start | bytes 393224 | tf_op jit(solution)/shard_map/while/body/eval_jaxpr/ppermute | solution.py:12
  257.0 14.1 %collective-permute-start = (bf16[512,128]{1,0:T(8,128)(2,1)}, bf16[512,128]{1,0:T(8,128)(2,1)}, u32[]{:S(2)}, u32[]{:S(2)}) collective-permute-start(bf16[512,128]{1,0:T(8,128)(2,1)} %get-tuple-element.88), channel_id=1, source_target_pairs={{31,0},{0,1},{1,2},{2,3},{3,4},{4,5},{5,6},{6,7},{7,8},{8,9},{9,10... | collective-permute-start | bytes 393224 | tf_op jit(solution)/shard_map/while/body/eval_jaxpr/ppermute | solution.py:12
  259.9 23.8 %collective-permute-start.2 = (bf16[256,768]{1,0:T(8,128)(2,1)S(1)}, bf16[256,768]{1,0:T(8,128)(2,1)}, u32[]{:S(2)}, u32[]{:S(2)}) collective-permute-start(bf16[256,768]{1,0:T(8,128)(2,1)S(1)} %copy.23), channel_id=1, source_target_pairs={{480,0},{0,32},{32,64},{64,96},{96,128},{128,160},{160,192},{192,2... | collective-permute-start | bytes 1179656 | tf_op jit(solution)/shard_map/while/body/eval_jaxpr/ppermute | solution.py:12
  271.1 12.6 %collective-permute-start.1 = (bf16[512,128]{1,0:T(8,128)(2,1)}, bf16[512,128]{1,0:T(8,128)(2,1)}, u32[]{:S(2)}, u32[]{:S(2)}) collective-permute-start(bf16[512,128]{1,0:T(8,128)(2,1)} %collective-permute-done), channel_id=1, source_target_pairs={{31,0},{0,1},{1,2},{2,3},{3,4},{4,5},{5,6},{6,7},{7,8},{8,9},{9,10... | collective-permute-start | bytes 393224 | tf_op jit(solution)/shard_map/while/body/eval_jaxpr/ppermute | solution.py:12
  283.7 14.1 %collective-permute-start = (bf16[512,128]{1,0:T(8,128)(2,1)}, bf16[512,128]{1,0:T(8,128)(2,1)}, u32[]{:S(2)}, u32[]{:S(2)}) collective-permute-start(bf16[512,128]{1,0:T(8,128)(2,1)} %get-tuple-element.88), channel_id=1, source_target_pairs={{31,0},{0,1},{1,2},{2,3},{3,4},{4,5},{5,6},{6,7},{7,8},{8,9},{9,10... | collective-permute-start | bytes 393224 | tf_op jit(solution)/shard_map/while/body/eval_jaxpr/ppermute | solution.py:12
  286.6 23.8 %collective-permute-start.2 = (bf16[256,768]{1,0:T(8,128)(2,1)S(1)}, bf16[256,768]{1,0:T(8,128)(2,1)}, u32[]{:S(2)}, u32[]{:S(2)}) collective-permute-start(bf16[256,768]{1,0:T(8,128)(2,1)S(1)} %copy.23), channel_id=1, source_target_pairs={{480,0},{0,32},{32,64},{64,96},{96,128},{128,160},{160,192},{192,2... | collective-permute-start | bytes 1179656 | tf_op jit(solution)/shard_map/while/body/eval_jaxpr/ppermute | solution.py:12
  297.8 12.6 %collective-permute-start.1 = (bf16[512,128]{1,0:T(8,128)(2,1)}, bf16[512,128]{1,0:T(8,128)(2,1)}, u32[]{:S(2)}, u32[]{:S(2)}) collective-permute-start(bf16[512,128]{1,0:T(8,128)(2,1)} %collective-permute-done), channel_id=1, source_target_pairs={{31,0},{0,1},{1,2},{2,3},{3,4},{4,5},{5,6},{6,7},{7,8},{8,9},{9,10... | collective-permute-start | bytes 393224 | tf_op jit(solution)/shard_map/while/body/eval_jaxpr/ppermute | solution.py:12
  310.4 14.1 %collective-permute-start = (bf16[512,128]{1,0:T(8,128)(2,1)}, bf16[512,128]{1,0:T(8,128)(2,1)}, u32[]{:S(2)}, u32[]{:S(2)}) collective-permute-start(bf16[512,128]{1,0:T(8,128)(2,1)} %get-tuple-element.88), channel_id=1, source_target_pairs={{31,0},{0,1},{1,2},{2,3},{3,4},{4,5},{5,6},{6,7},{7,8},{8,9},{9,10... | collective-permute-start | bytes 393224 | tf_op jit(solution)/shard_map/while/body/eval_jaxpr/ppermute | solution.py:12
  313.3 23.8 %collective-permute-start.2 = (bf16[256,768]{1,0:T(8,128)(2,1)S(1)}, bf16[256,768]{1,0:T(8,128)(2,1)}, u32[]{:S(2)}, u32[]{:S(2)}) collective-permute-start(bf16[256,768]{1,0:T(8,128)(2,1)S(1)} %copy.23), channel_id=1, source_target_pairs={{480,0},{0,32},{32,64},{64,96},{96,128},{128,160},{160,192},{192,2... | collective-permute-start | bytes 1179656 | tf_op jit(solution)/shard_map/while/body/eval_jaxpr/ppermute | solution.py:12
  324.5 12.6 %collective-permute-start.1 = (bf16[512,128]{1,0:T(8,128)(2,1)}, bf16[512,128]{1,0:T(8,128)(2,1)}, u32[]{:S(2)}, u32[]{:S(2)}) collective-permute-start(bf16[512,128]{1,0:T(8,128)(2,1)} %collective-permute-done), channel_id=1, source_target_pairs={{31,0},{0,1},{1,2},{2,3},{3,4},{4,5},{5,6},{6,7},{7,8},{8,9},{9,10... | collective-permute-start | bytes 393224 | tf_op jit(solution)/shard_map/while/body/eval_jaxpr/ppermute | solution.py:12
  337.1 14.1 %collective-permute-start = (bf16[512,128]{1,0:T(8,128)(2,1)}, bf16[512,128]{1,0:T(8,128)(2,1)}, u32[]{:S(2)}, u32[]{:S(2)}) collective-permute-start(bf16[512,128]{1,0:T(8,128)(2,1)} %get-tuple-element.88), channel_id=1, source_target_pairs={{31,0},{0,1},{1,2},{2,3},{3,4},{4,5},{5,6},{6,7},{7,8},{8,9},{9,10... | collective-permute-start | bytes 393224 | tf_op jit(solution)/shard_map/while/body/eval_jaxpr/ppermute | solution.py:12
  340.0 23.8 %collective-permute-start.2 = (bf16[256,768]{1,0:T(8,128)(2,1)S(1)}, bf16[256,768]{1,0:T(8,128)(2,1)}, u32[]{:S(2)}, u32[]{:S(2)}) collective-permute-start(bf16[256,768]{1,0:T(8,128)(2,1)S(1)} %copy.23), channel_id=1, source_target_pairs={{480,0},{0,32},{32,64},{64,96},{96,128},{128,160},{160,192},{192,2... | collective-permute-start | bytes 1179656 | tf_op jit(solution)/shard_map/while/body/eval_jaxpr/ppermute | solution.py:12
  351.2 12.6 %collective-permute-start.1 = (bf16[512,128]{1,0:T(8,128)(2,1)}, bf16[512,128]{1,0:T(8,128)(2,1)}, u32[]{:S(2)}, u32[]{:S(2)}) collective-permute-start(bf16[512,128]{1,0:T(8,128)(2,1)} %collective-permute-done), channel_id=1, source_target_pairs={{31,0},{0,1},{1,2},{2,3},{3,4},{4,5},{5,6},{6,7},{7,8},{8,9},{9,10... | collective-permute-start | bytes 393224 | tf_op jit(solution)/shard_map/while/body/eval_jaxpr/ppermute | solution.py:12
  363.8 14.1 %collective-permute-start = (bf16[512,128]{1,0:T(8,128)(2,1)}, bf16[512,128]{1,0:T(8,128)(2,1)}, u32[]{:S(2)}, u32[]{:S(2)}) collective-permute-start(bf16[512,128]{1,0:T(8,128)(2,1)} %get-tuple-element.88), channel_id=1, source_target_pairs={{31,0},{0,1},{1,2},{2,3},{3,4},{4,5},{5,6},{6,7},{7,8},{8,9},{9,10... | collective-permute-start | bytes 393224 | tf_op jit(solution)/shard_map/while/body/eval_jaxpr/ppermute | solution.py:12
  366.7 23.8 %collective-permute-start.2 = (bf16[256,768]{1,0:T(8,128)(2,1)S(1)}, bf16[256,768]{1,0:T(8,128)(2,1)}, u32[]{:S(2)}, u32[]{:S(2)}) collective-permute-start(bf16[256,768]{1,0:T(8,128)(2,1)S(1)} %copy.23), channel_id=1, source_target_pairs={{480,0},{0,32},{32,64},{64,96},{96,128},{128,160},{160,192},{192,2... | collective-permute-start | bytes 1179656 | tf_op jit(solution)/shard_map/while/body/eval_jaxpr/ppermute | solution.py:12
  377.9 12.6 %collective-permute-start.1 = (bf16[512,128]{1,0:T(8,128)(2,1)}, bf16[512,128]{1,0:T(8,128)(2,1)}, u32[]{:S(2)}, u32[]{:S(2)}) collective-permute-start(bf16[512,128]{1,0:T(8,128)(2,1)} %collective-permute-done), channel_id=1, source_target_pairs={{31,0},{0,1},{1,2},{2,3},{3,4},{4,5},{5,6},{6,7},{7,8},{8,9},{9,10... | collective-permute-start | bytes 393224 | tf_op jit(solution)/shard_map/while/body/eval_jaxpr/ppermute | solution.py:12
  390.5 14.1 %collective-permute-start = (bf16[512,128]{1,0:T(8,128)(2,1)}, bf16[512,128]{1,0:T(8,128)(2,1)}, u32[]{:S(2)}, u32[]{:S(2)}) collective-permute-start(bf16[512,128]{1,0:T(8,128)(2,1)} %get-tuple-element.88), channel_id=1, source_target_pairs={{31,0},{0,1},{1,2},{2,3},{3,4},{4,5},{5,6},{6,7},{7,8},{8,9},{9,10... | collective-permute-start | bytes 393224 | tf_op jit(solution)/shard_map/while/body/eval_jaxpr/ppermute | solution.py:12
  393.4 23.8 %collective-permute-start.2 = (bf16[256,768]{1,0:T(8,128)(2,1)S(1)}, bf16[256,768]{1,0:T(8,128)(2,1)}, u32[]{:S(2)}, u32[]{:S(2)}) collective-permute-start(bf16[256,768]{1,0:T(8,128)(2,1)S(1)} %copy.23), channel_id=1, source_target_pairs={{480,0},{0,32},{32,64},{64,96},{96,128},{128,160},{160,192},{192,2... | collective-permute-start | bytes 1179656 | tf_op jit(solution)/shard_map/while/body/eval_jaxpr/ppermute | solution.py:12
  404.6 12.6 %collective-permute-start.1 = (bf16[512,128]{1,0:T(8,128)(2,1)}, bf16[512,128]{1,0:T(8,128)(2,1)}, u32[]{:S(2)}, u32[]{:S(2)}) collective-permute-start(bf16[512,128]{1,0:T(8,128)(2,1)} %collective-permute-done), channel_id=1, source_target_pairs={{31,0},{0,1},{1,2},{2,3},{3,4},{4,5},{5,6},{6,7},{7,8},{8,9},{9,10... | collective-permute-start | bytes 393224 | tf_op jit(solution)/shard_map/while/body/eval_jaxpr/ppermute | solution.py:12
  417.2 14.1 %collective-permute-start = (bf16[512,128]{1,0:T(8,128)(2,1)}, bf16[512,128]{1,0:T(8,128)(2,1)}, u32[]{:S(2)}, u32[]{:S(2)}) collective-permute-start(bf16[512,128]{1,0:T(8,128)(2,1)} %get-tuple-element.88), channel_id=1, source_target_pairs={{31,0},{0,1},{1,2},{2,3},{3,4},{4,5},{5,6},{6,7},{7,8},{8,9},{9,10... | collective-permute-start | bytes 393224 | tf_op jit(solution)/shard_map/while/body/eval_jaxpr/ppermute | solution.py:12
  420.1 23.8 %collective-permute-start.2 = (bf16[256,768]{1,0:T(8,128)(2,1)S(1)}, bf16[256,768]{1,0:T(8,128)(2,1)}, u32[]{:S(2)}, u32[]{:S(2)}) collective-permute-start(bf16[256,768]{1,0:T(8,128)(2,1)S(1)} %copy.23), channel_id=1, source_target_pairs={{480,0},{0,32},{32,64},{64,96},{96,128},{128,160},{160,192},{192,2... | collective-permute-start | bytes 1179656 | tf_op jit(solution)/shard_map/while/body/eval_jaxpr/ppermute | solution.py:12
  431.3 12.6 %collective-permute-start.1 = (bf16[512,128]{1,0:T(8,128)(2,1)}, bf16[512,128]{1,0:T(8,128)(2,1)}, u32[]{:S(2)}, u32[]{:S(2)}) collective-permute-start(bf16[512,128]{1,0:T(8,128)(2,1)} %collective-permute-done), channel_id=1, source_target_pairs={{31,0},{0,1},{1,2},{2,3},{3,4},{4,5},{5,6},{6,7},{7,8},{8,9},{9,10... | collective-permute-start | bytes 393224 | tf_op jit(solution)/shard_map/while/body/eval_jaxpr/ppermute | solution.py:12
where the time goes:
time: 454 us; the launch traced here: 451 us
  waiting for transfers between devices  286 us (63%)
  starting transfers between devices  93.3 us (21%)
  matrix products  41.3 us (9%)
  local copies, waits for them, and re-layouts  24.1 us (5%)
  other arithmetic  5.18 us (1%)
    ppermute x48, waiting for transfers between devices, passed_along(): return lax.ppermute(block, axis, route)  286 us
    ppermute x48, starting transfers between devices, passed_along(): return lax.ppermute(block, axis, route)  93.3 us
    dot_general x32, matrix products, outer_step(): jnp.dot(a_current, b_rows, preferred_element_type=jnp.float32)  40.4 us
    while x16, local copies, waits for them, and re-layouts  16 us
  transfers between devices with their start and end apart: 48, of which 32 were waited for; matrix products, arithmetic and copies ran while one was open for 12% of the time, Pallas kernels for 0%

commit v1 on v0

v1 whole, which is shorter than its diff:
```python
import jax
import jax.numpy as jnp
from jax import lax
from jax.experimental import pallas as pl
from jax.experimental.pallas import tpu as pltpu
from jax.sharding import PartitionSpec as P

TILE = 64
NX, NY, NH, NZ = 4, 4, 2, 8
MESH = pl.DeviceIdType.MESH


def kernel(a_ref, b_ref, out_ref, a_all, b_all, acc, a_recv, b_recv, core_send, z_send, h_send,
           y_send, x_send, f_send):
    row = lax.axis_index("row")
    col = lax.axis_index("col")
    x, y = row // NY, row % NY
    core, z, h = col % 2, (col // 2) % NZ, col // (2 * NZ)

    def row_at(xi, yi):
        return xi * NY + yi

    def col_at(hi, zi, ci):
        return (hi * NZ + zi) * 2 + ci

    x_next, x_prev, x_far = (x + 1) % NX, (x + NX - 1) % NX, (x + 2) % NX
    to_x = ((row_at(x_next, y), col), (row_at(x_prev, y), col))
    to_y = ((row_at(x, (y + 1) % NY), col), (row_at(x, (y + NY - 1) % NY), col))
    to_z = ((row, col_at(h, (z + 1) % NZ, core)), (row, col_at(h, (z + NZ - 1) % NZ, core)))
    to_core = (row, col_at(h, z, 1 - core))
    to_h = (row, col_at(1 - h, z, core))

    barrier = pltpu.get_barrier_semaphore()
    partners = (*to_x, *to_y, *to_z, to_core, to_h)
    for partner in partners:
        pl.semaphore_signal(barrier, inc=1, device_id=partner, device_id_type=MESH)
    pl.semaphore_wait(barrier, len(partners))

    def a_copy(source, q, send, to):
        return pltpu.make_async_remote_copy(
            src_ref=source, dst_ref=a_all.at[q], send_sem=send, recv_sem=a_recv.at[q],
            device_id=to, device_id_type=MESH)

    def b_copy(source, panel, send, to):
        return pltpu.make_async_remote_copy(
            src_ref=source, dst_ref=b_all.at[panel], send_sem=send, recv_sem=b_recv.at[panel],
            device_id=to, device_id_type=MESH)

    def a_arrived(q):
        a_copy(a_all.at[q], q, core_send.at[0], to_core).wait_recv()

    def b_arrived(panel):
        b_copy(b_all.at[panel], panel, x_send.at[0, 0, 0], to_x[0]).wait_recv()

    def panel_at(xi, yi, p):
        return row_at(xi, yi) * 2 + p

    def own_b(p):
        return b_ref.at[pl.ds(p * 128, 128)]

    def y_copy(source, yi, p, way):
        return b_copy(source, panel_at(x, yi, p), y_send.at[way, yi, p], to_y[way])

    def x_copy(source, yi, p, way):
        return b_copy(source, panel_at(x, yi, p), x_send.at[way, yi, p], to_x[way])

    a_hops = ((4, 3), (3, 4))

    def z_copy(source, q, kind, way, hop):
        return a_copy(source, q, z_send.at[kind, way, hop], to_z[way])

    def core_copy(source, q, zi, kind):
        return a_copy(source, q, core_send.at[kind * NZ + zi], to_core)

    a_copy(a_ref, col, h_send, to_h).start()
    z_copy(a_ref, col, 0, 0, 0).start()
    z_copy(a_ref, col, 0, 1, 0).start()
    for p in (0, 1):
        @pl.when(y < NY - 1)
        def _(p=p):
            y_copy(own_b(p), y, p, 0).start()

        @pl.when(y > 0)
        def _(p=p):
            y_copy(own_b(p), y, p, 1).start()

        x_copy(own_b(p), y, p, 0).start()
        x_copy(own_b(1 - p), y, 1 - p, 1).start()
    core_copy(a_ref, col, z, 0).start()

    a_all[col] = a_ref[...]
    b_all[row * 2] = b_ref[:128]
    b_all[row * 2 + 1] = b_ref[128:]
    acc[...] = jnp.zeros_like(acc)

    def a_step(kind, step):
        half = h if kind == 0 else 1 - h
        for way in (0, 1):
            if step <= a_hops[kind][way]:
                zi = (z + (NZ - step if way == 0 else step)) % NZ
                q = col_at(half, zi, core)
                a_arrived(q)
                if step < a_hops[kind][way]:
                    z_copy(a_all.at[q], q, kind, way, step).start()
                core_copy(a_all.at[q], q, zi, kind).start()

    def a_other_half():
        q = col_at(1 - h, z, core)
        a_arrived(q)
        z_copy(a_all.at[q], q, 1, 0, 0).start()
        z_copy(a_all.at[q], q, 1, 1, 0).start()
        core_copy(a_all.at[q], q, z, 1).start()

    def y_step(step):
        for way in (0, 1):
            yi = y - step if way == 0 else y + step

            @pl.when((yi >= 0) & (yi < NY))
            def _(yi=yi, way=way):
                for p in (0, 1):
                    panel = panel_at(x, yi, p)
                    b_arrived(panel)

                    @pl.when((y < NY - 1) if way == 0 else (y > 0))
                    def _():
                        y_copy(b_all.at[panel], yi, p, way).start()

                    x_copy(b_all.at[panel], yi, p, 0).start()
                    x_copy(b_all.at[panel], yi, p, 1).start()

    order = (
        y,
        jnp.where(y == 0, 1, y - 1),
        jnp.where(y <= 1, 2, jnp.where(y == 2, 3, 1)),
        jnp.where(y <= 1, 3, 0),
    )

    def f_copy(k, way):
        panel = panel_at(x_prev if way == 0 else x_next, order[k], way)
        return b_copy(b_all.at[panel], panel, f_send.at[way, k], to_x[way])

    def x_forward(k):
        b_arrived(panel_at(x_prev, order[k], 0))
        f_copy(k, 0).start()
        b_arrived(panel_at(x_next, order[k], 1))
        f_copy(k, 1).start()

    def multiply(k):
        yi = order[k]
        b_arrived(panel_at(x_prev, yi, 1))
        b_arrived(panel_at(x_next, yi, 0))
        b_arrived(panel_at(x_far, yi, 0))
        b_arrived(panel_at(x_far, yi, 1))

        @pl.loop(0, NX)
        def _(xi):
            first = row_at(xi, yi) * 2
            shift = first + col + 64 - 2 * row - 1
            a_two = jnp.concatenate([a_all[shift % 32], a_all[(shift + 1) % 32]], axis=1)
            for n in range(3):
                cols = pl.ds(n * 256, 256)
                b_two = jnp.concatenate([b_all[first, :, cols], b_all[first + 1, :, cols]], axis=0)
                acc[:, cols] += jnp.dot(a_two, b_two, preferred_element_type=jnp.float32)

    a_step(0, 1)
    y_step(1)
    x_forward(0)
    a_other_half()
    a_step(0, 2)
    a_step(1, 1)
    y_step(2)
    x_forward(1)
    a_step(0, 3)
    a_step(1, 2)
    y_step(3)
    a_step(0, 4)
    a_step(1, 3)
    x_forward(2)
    a_step(1, 4)
    for half in range(NH):
        for zi in range(NZ):
            a_arrived(col_at(half, zi, 1 - core))
    multiply(0)
    multiply(1)
    x_forward(3)
    multiply(2)
    multiply(3)
    out_ref[...] = acc[...].astype(out_ref.dtype)

    a_copy(a_ref, col, h_send, to_h).wait_send()
    for kind in (0, 1):
        for way in (0, 1):
            for hop in range(a_hops[kind][way]):
                z_copy(a_ref, col, kind, way, hop).wait_send()
        for zi in range(NZ):
            core_copy(a_ref, col, zi, kind).wait_send()
    for p in (0, 1):
        for yi in range(NY):
            @pl.when((y < NY - 1) & (yi <= y))
            def _(yi=yi, p=p):
                y_copy(own_b(p), yi, p, 0).wait_send()

            @pl.when((y > 0) & (yi >= y))
            def _(yi=yi, p=p):
                y_copy(own_b(p), yi, p, 1).wait_send()

            for way in (0, 1):
                x_copy(own_b(p), yi, p, way).wait_send()
    for k in range(NY):
        for way in (0, 1):
            f_copy(k, way).wait_send()


def per_device(row_ids, a_tiles, a_mask, b_tiles, b_mask, c_keep):
    def by_blocks(array, blocks):
        wide = jnp.repeat(blocks, TILE, axis=1).astype(array.dtype)
        tall = array.reshape(blocks.shape[0], TILE, array.shape[1])
        return (tall * wide[:, None, :]).reshape(array.shape)

    a_eff = by_blocks(a_tiles, a_mask)
    b_eff = by_blocks(b_tiles, b_mask)
    dma = pltpu.SemaphoreType.DMA
    product = pl.pallas_call(
        kernel,
        out_shape=jax.ShapeDtypeStruct((512, 768), jnp.bfloat16),
        in_specs=[pl.BlockSpec(memory_space=pltpu.VMEM)] * 2,
        out_specs=pl.BlockSpec(memory_space=pltpu.VMEM),
        scratch_shapes=[
            pltpu.VMEM((32, 512, 128), jnp.bfloat16),
            pltpu.VMEM((32, 128, 768), jnp.bfloat16),
            pltpu.VMEM((512, 768), jnp.float32),
            dma((32,)),
            dma((32,)),
            dma((16,)),
            dma((2, 2, 4)),
            dma,
            dma((2, NY, 2)),
            dma((2, NY, 2)),
            dma((2, NY)),
        ],
        compiler_params=pltpu.CompilerParams(collective_id=0, has_side_effects=True),
    )(a_eff, b_eff)
    onehot = (row_ids[:, None] == jnp.arange(c_keep.shape[0], dtype=jnp.int32)[None, :]).astype(
        jnp.float32
    )
    keep = jnp.dot(onehot, c_keep.astype(jnp.float32))
    return by_blocks(product, keep)


def solution(mesh):
    placed = (
        P("row"),
        P("row", "col"),
        P("row", "col"),
        P("row", "col"),
        P("row", "col"),
        P(None, "col"),
    )
    return jax.shard_map(
        per_device, mesh=mesh, in_specs=placed, out_specs=P("row", "col"), check_vma=False
    )
```

time: 454 us -> 78.1 us (0.17)
  the two profiles are of different devices: /device:TPU:8 before, /device:TPU:1 now
where the time goes in v1:
time: 78.1 us; the launch traced here: 77.3 us
  Pallas kernels  71.2 us (91%)
  other arithmetic  5.23 us (7%)
    pallas_call x1, Pallas kernels, per_device(): pl.pallas_call(kernel, out_shape=jax.ShapeDtypeStruct((512, 768), jnp.bfl...  71.2 us
    mul x3, other arithmetic, by_blocks(): return (tall * wide[:, None, :]).reshape(array.shape)  4.54 us

profile of v1, /device:TPU:1, one launch (start us, length us, event | category | flops | bytes accessed | tf_op | source)
XLA Modules:
  0.0 77.3 jit_solution(3850907653937274806)
XLA Ops:
  0.0 0.7 convert_element_type.39
  0.7 0.1 broadcast_in_dim.7
  0.8 0.1 convert_element_type.40
  0.9 0.0 copy-start.2
  0.9 0.0 copy-start
  0.9 1.8 %bitcast_multiply_fusion.1.b_ref = bf16[256,768]{1,0:T(8,128)(2,1)} fusion(bf16[256,768]{1,0:T(8,128)(2,1)} %param.9, bf16[4,768]{1,0:T(4,128)(2,1)S(1)} %convert_element_type.40), kind=kLoop, calls=%fused_computation.2 | loop fusion | flops 196608 | bytes 792576 | tf_op jit(solution)/shard_map/mul | solution.py:218
  2.7 0.0 copy-done.2
  2.7 0.1 copy.8
  2.8 0.1 broadcast_in_dim.6
  2.9 0.1 convert_element_type.38
  2.9 0.0 copy-done
  2.9 0.7 bitcast_multiply_fusion.2.a_ref
  3.6 0.0 copy-start.1
  3.6 0.0 copy-start.3
  3.6 71.2 %shard_map.64 = bf16[512,768]{1,0:T(8,128)(2,1)} custom-call(bf16[512,128]{1,0:T(8,128)(2,1)} %bitcast_multiply_fusion.2.a_ref, bf16[256,768]{1,0:T(8,128)(2,1)} %bitcast_multiply_fusion.1.b_ref), custom_call_target="tpu_custom_call" | custom-call | tf_op jit(solution)/shard_map/pallas_call | solution.py:223
  74.8 0.0 copy-done.1
  74.8 0.0 copy-done.3
  74.8 0.2 convolution_convert_fusion
  75.0 0.1 broadcast_in_dim.16
  75.1 0.1 convert_element_type.43
  75.2 2.1 %bitcast_multiply_fusion = bf16[512,768]{1,0:T(8,128)(2,1)} fusion(bf16[512,768]{1,0:T(8,128)(2,1)} %shard_map.64, bf16[8,768]{1,0:T(8,128)(2,1)S(1)} %convert_element_type.43), kind=kLoop, calls=%fused_computation.1 | loop fusion | flops 393216 | bytes 1585152 | tf_op jit(solution)/shard_map/mul | solution.py:218
  (1 shorter events, 0.0 us)
Async XLA Ops:
  0.9 1.8 %copy-start.2 = (s32[8,2]{0,1:T(2,128)S(1)}, s32[8,2]{0,1:T(2,128)}, u32[]{:S(2)}) copy-start(s32[8,2]{0,1:T(2,128)} %param.8) | copy-start | bytes 196
  0.9 2.1 %copy-start = (bf16[512,128]{1,0:T(8,128)(2,1)S(1)}, bf16[512,128]{1,0:T(8,128)(2,1)}, u32[]{:S(2)}) copy-start(bf16[512,128]{1,0:T(8,128)(2,1)} %param.7) | copy-start | bytes 393220
  3.6 71.2 %copy-start.1 = (s32[128,12]{0,1:T(8,128)S(1)}, s32[128,12]{0,1:T(8,128)}, u32[]{:S(2)}) copy-start(s32[128,12]{0,1:T(8,128)} %param.11) | copy-start | bytes 18436
  3.6 71.2 %copy-start.3 = (s32[8]{0:T(128)S(1)}, s32[8]{0:T(128)}, u32[]{:S(2)}) copy-start(s32[8]{0:T(128)} %param.6) | copy-start | bytes 100

commit v2 on v1

v2 whole, which is shorter than its diff:
```python
import jax
import jax.numpy as jnp
from jax import lax
from jax.experimental import pallas as pl
from jax.experimental.pallas import tpu as pltpu
from jax.sharding import PartitionSpec as P

TILE = 64
NX, NY, NH, NZ = 4, 4, 2, 8
MAIN, EDGE = 112, 16
MESH = pl.DeviceIdType.MESH


def kernel(a_ref, b_ref, out_ref, a_all, b_all, acc, a_recv, b_recv, e_recv, u_recv, core_send, z_send,
           h_send, y_send, x_send, f_send, e_send, ef_send, u_send, local_sem):
    row = lax.axis_index("row")
    col = lax.axis_index("col")
    x, y = row // NY, row % NY
    core, z, h = col % 2, (col // 2) % NZ, col // (2 * NZ)

    def row_at(xi, yi):
        return xi * NY + yi

    def col_at(hi, zi, ci):
        return (hi * NZ + zi) * 2 + ci

    x_next, x_prev, x_far = (x + 1) % NX, (x + NX - 1) % NX, (x + 2) % NX
    to_x = ((row_at(x_next, y), col), (row_at(x_prev, y), col))
    to_y = ((row_at(x, (y + 1) % NY), col), (row_at(x, (y + NY - 1) % NY), col))
    to_z = ((row, col_at(h, (z + 1) % NZ, core)), (row, col_at(h, (z + NZ - 1) % NZ, core)))
    to_core = (row, col_at(h, z, 1 - core))
    to_h = (row, col_at(1 - h, z, core))

    barrier = pltpu.get_barrier_semaphore()
    partners = (*to_x, *to_y, *to_z, to_core, to_h)
    for partner in partners:
        pl.semaphore_signal(barrier, inc=1, device_id=partner, device_id_type=MESH)
    pl.semaphore_wait(barrier, len(partners))

    def send(source, target, send_sem, recv_sem, to):
        return pltpu.make_async_remote_copy(
            src_ref=source, dst_ref=target, send_sem=send_sem, recv_sem=recv_sem,
            device_id=to, device_id_type=MESH)

    def arrived(target, recv_sem):
        send(target, target, h_send, recv_sem, to_core).wait_recv()

    def a_copy(source, q, send_sem, to):
        return send(source, a_all.at[q], send_sem, a_recv.at[q], to)

    def a_arrived(q):
        arrived(a_all.at[q], a_recv.at[q])

    def main(xi, yi, p):
        return b_all.at[xi, yi, pl.ds(p * MAIN, MAIN)]

    def edge(xi, yi, p):
        return b_all.at[xi, yi, pl.ds(2 * MAIN + p * EDGE, EDGE)]

    def bundle(yi):
        return b_all.at[:, yi, pl.ds(2 * MAIN, 2 * EDGE)]

    def main_copy(source, xi, yi, p, send_sem, to):
        return send(source, main(xi, yi, p), send_sem, b_recv.at[xi, yi, p], to)

    def main_arrived(xi, yi, p):
        arrived(main(xi, yi, p), b_recv.at[xi, yi, p])

    def edge_arrived(xi, p):
        arrived(edge(xi, y, p), e_recv.at[xi, p])

    def own_main(p):
        return b_ref.at[pl.ds(p * MAIN, MAIN)]

    def own_edge(p):
        return b_ref.at[pl.ds(2 * MAIN + p * EDGE, EDGE)]

    def y_copy(source, yi, p, way):
        return main_copy(source, x, yi, p, y_send.at[way, yi, p], to_y[way])

    def x_copy(source, yi, p, way):
        return main_copy(source, x, yi, p, x_send.at[way, yi, p], to_x[way])

    def e_copy(p, way):
        return send(own_edge(p), edge(x, y, p), e_send.at[way, p], e_recv.at[x, p], to_x[way])

    def e_forward(way):
        xi = x_prev if way == 0 else x_next
        return send(edge(xi, y, way), edge(xi, y, way), ef_send.at[way], e_recv.at[xi, way], to_x[way])

    def u_copy(yi, way):
        return send(bundle(yi), bundle(yi), u_send.at[way, yi], u_recv.at[yi], to_y[way])

    a_hops = ((4, 3), (3, 4))

    def z_copy(source, q, kind, way, hop):
        return a_copy(source, q, z_send.at[kind, way, hop], to_z[way])

    def core_copy(source, q, zi, kind):
        return a_copy(source, q, core_send.at[kind * NZ + zi], to_core)

    def further(way):
        return (y < NY - 1) if way == 0 else (y > 0)

    for p in (0, 1):
        e_copy(p, 0).start()
        e_copy(1 - p, 1).start()
    for p in (0, 1):
        for way in (0, 1):
            @pl.when(further(way))
            def _():
                y_copy(own_main(p), y, p, way).start()

        x_copy(own_main(p), y, p, 0).start()
        x_copy(own_main(1 - p), y, 1 - p, 1).start()
    z_copy(a_ref, col, 0, 0, 0).start()
    z_copy(a_ref, col, 0, 1, 0).start()
    a_copy(a_ref, col, h_send, to_h).start()
    core_copy(a_ref, col, z, 0).start()
    local = pltpu.make_async_copy(b_ref, b_all.at[x, y], local_sem)
    local.start()

    a_all[col] = a_ref[...]
    acc[...] = jnp.zeros_like(acc)

    def a_step(kind, step):
        half = h if kind == 0 else 1 - h
        for way in (0, 1):
            if step <= a_hops[kind][way]:
                zi = (z + (NZ - step if way == 0 else step)) % NZ
                q = col_at(half, zi, core)
                a_arrived(q)
                if step < a_hops[kind][way]:
                    z_copy(a_all.at[q], q, kind, way, step).start()
                core_copy(a_all.at[q], q, zi, kind).start()

    def a_other_half():
        q = col_at(1 - h, z, core)
        a_arrived(q)
        z_copy(a_all.at[q], q, 1, 0, 0).start()
        z_copy(a_all.at[q], q, 1, 1, 0).start()
        core_copy(a_all.at[q], q, z, 1).start()

    def y_step(step):
        for way in (0, 1):
            yi = y - step if way == 0 else y + step

            @pl.when((yi >= 0) & (yi < NY))
            def _(yi=yi, way=way):
                for p in (0, 1):
                    main_arrived(x, yi, p)

                    @pl.when(further(way))
                    def _():
                        y_copy(main(x, yi, p), yi, p, way).start()

                    x_copy(main(x, yi, p), yi, p, 0).start()
                    x_copy(main(x, yi, p), yi, p, 1).start()

    def u_step(step):
        for way in (0, 1):
            yi = y - step if way == 0 else y + step

            @pl.when((yi >= 0) & (yi < NY))
            def _(yi=yi, way=way):
                arrived(bundle(yi), u_recv.at[yi])

                @pl.when(further(way))
                def _():
                    u_copy(yi, way).start()

    def edges_forward():
        edge_arrived(x_prev, 0)
        e_forward(0).start()
        edge_arrived(x_next, 1)
        e_forward(1).start()

    def own_bundle():
        local.wait()
        edge_arrived(x_prev, 1)
        edge_arrived(x_next, 0)
        edge_arrived(x_far, 0)
        edge_arrived(x_far, 1)
        for way in (0, 1):
            @pl.when(further(way))
            def _():
                u_copy(y, way).start()

    order = (
        y,
        jnp.where(y == 0, 1, y - 1),
        jnp.where(y <= 1, 2, jnp.where(y == 2, 3, 1)),
        jnp.where(y <= 1, 3, 0),
    )

    def f_copy(k, way):
        xi = x_prev if way == 0 else x_next
        return main_copy(main(xi, order[k], way), xi, order[k], way, f_send.at[way, k], to_x[way])

    def x_forward(k):
        main_arrived(x_prev, order[k], 0)
        f_copy(k, 0).start()
        main_arrived(x_next, order[k], 1)
        f_copy(k, 1).start()

    def add_block(xi, yi):
        shift = row_at(xi, yi) * 2 + col + 64 - 2 * row - 1
        a_two = jnp.concatenate([a_all[shift % 32], a_all[(shift + 1) % 32]], axis=1)
        for n in range(3):
            cols = pl.ds(n * 256, 256)
            acc[:, cols] += jnp.dot(a_two, b_all[xi, yi, :, cols], preferred_element_type=jnp.float32)

    def multiply(k):
        yi = order[k]
        main_arrived(x_prev, yi, 1)
        main_arrived(x_next, yi, 0)

        @pl.loop(0, 3)
        def _(j):
            add_block((x + NX - 1 + j) % NX, yi)

        main_arrived(x_far, yi, 0)
        main_arrived(x_far, yi, 1)
        add_block(x_far, yi)

    edges_forward()
    a_step(0, 1)
    x_forward(0)
    y_step(1)
    own_bundle()
    a_step(0, 2)
    x_forward(1)
    a_other_half()
    y_step(2)
    a_step(0, 3)
    a_step(1, 1)
    u_step(1)
    x_forward(2)
    y_step(3)
    a_step(0, 4)
    a_step(1, 2)
    u_step(2)
    a_step(1, 3)
    a_step(1, 4)
    for half in range(NH):
        for zi in range(NZ):
            a_arrived(col_at(half, zi, 1 - core))
    multiply(0)
    multiply(1)
    x_forward(3)
    multiply(2)
    u_step(3)
    multiply(3)
    out_ref[...] = acc[...].astype(out_ref.dtype)

    a_copy(a_ref, col, h_send, to_h).wait_send()
    for kind in (0, 1):
        for way in (0, 1):
            for hop in range(a_hops[kind][way]):
                z_copy(a_ref, col, kind, way, hop).wait_send()
        for zi in range(NZ):
            core_copy(a_ref, col, zi, kind).wait_send()
    for way in (0, 1):
        for p in (0, 1):
            e_copy(p, way).wait_send()
        e_forward(way).wait_send()
        for yi in range(NY):
            @pl.when(further(way) & ((yi <= y) if way == 0 else (yi >= y)))
            def _():
                y_copy(own_main(0), yi, 0, way).wait_send()
                y_copy(own_main(1), yi, 1, way).wait_send()
                u_copy(yi, way).wait_send()

            x_copy(own_main(0), yi, 0, way).wait_send()
            x_copy(own_main(1), yi, 1, way).wait_send()
            f_copy(yi, way).wait_send()


def per_device(row_ids, a_tiles, a_mask, b_tiles, b_mask, c_keep):
    def by_blocks(array, blocks):
        wide = jnp.repeat(blocks, TILE, axis=1).astype(array.dtype)
        tall = array.reshape(blocks.shape[0], TILE, array.shape[1])
        return (tall * wide[:, None, :]).reshape(array.shape)

    a_eff = by_blocks(a_tiles, a_mask)
    b_eff = by_blocks(b_tiles, b_mask)
    dma = pltpu.SemaphoreType.DMA
    product = pl.pallas_call(
        kernel,
        out_shape=jax.ShapeDtypeStruct((512, 768), jnp.bfloat16),
        in_specs=[pl.BlockSpec(memory_space=pltpu.VMEM)] * 2,
        out_specs=pl.BlockSpec(memory_space=pltpu.VMEM),
        scratch_shapes=[
            pltpu.VMEM((32, 512, 128), jnp.bfloat16),
            pltpu.VMEM((NX, NY, 256, 768), jnp.bfloat16),
            pltpu.VMEM((512, 768), jnp.float32),
            dma((32,)),
            dma((NX, NY, 2)),
            dma((NX, 2)),
            dma((NY,)),
            dma((16,)),
            dma((2, 2, 4)),
            dma,
            dma((2, NY, 2)),
            dma((2, NY, 2)),
            dma((2, NY)),
            dma((2, 2)),
            dma((2,)),
            dma((2, NY)),
            dma,
        ],
        compiler_params=pltpu.CompilerParams(collective_id=0, has_side_effects=True),
    )(a_eff, b_eff)
    onehot = (row_ids[:, None] == jnp.arange(c_keep.shape[0], dtype=jnp.int32)[None, :]).astype(
        jnp.float32
    )
    keep = jnp.dot(onehot, c_keep.astype(jnp.float32))
    return by_blocks(product, keep)


def solution(mesh):
    placed = (
        P("row"),
        P("row", "col"),
        P("row", "col"),
        P("row", "col"),
        P("row", "col"),
        P(None, "col"),
    )
    return jax.shard_map(
        per_device, mesh=mesh, in_specs=placed, out_specs=P("row", "col"), check_vma=False
    )
```

time: 78.1 us -> 74.9 us (0.959)
  Pallas kernels: 71.2 us -> 68.6 us
    pallas_call x1, Pallas kernels: 71.2 us -> 68.6 us  [per_device(): pl.pallas_call(kernel, out_shape=jax.ShapeDtypeStruct((512, 768), jnp.bfl...]
where the time goes in v2:
time: 74.9 us; the launch traced here: 74.7 us
  Pallas kernels  68.6 us (92%)
  other arithmetic  5.23 us (7%)
    pallas_call x1, Pallas kernels, per_device(): pl.pallas_call(kernel, out_shape=jax.ShapeDtypeStruct((512, 768), jnp.bfl...  68.6 us
    mul x3, other arithmetic, by_blocks(): return (tall * wide[:, None, :]).reshape(array.shape)  4.54 us

profile of v2, /device:TPU:1, one launch (start us, length us, event | category | flops | bytes accessed | tf_op | source)
XLA Modules:
  0.0 74.7 jit_solution(8448174566210404023)
XLA Ops:
  0.0 0.7 convert_element_type.39
  0.7 0.1 broadcast_in_dim.7
  0.8 0.1 convert_element_type.40
  0.9 0.0 copy-start.2
  0.9 0.0 copy-start
  0.9 1.8 %bitcast_multiply_fusion.1.b_ref = bf16[256,768]{1,0:T(8,128)(2,1)} fusion(bf16[256,768]{1,0:T(8,128)(2,1)} %param.9, bf16[4,768]{1,0:T(4,128)(2,1)S(1)} %convert_element_type.40), kind=kLoop, calls=%fused_computation.2 | loop fusion | flops 196608 | bytes 792576 | tf_op jit(solution)/shard_map/mul | solution.py:283
  2.7 0.0 copy-done.2
  2.7 0.1 copy.8
  2.8 0.1 broadcast_in_dim.6
  2.9 0.1 convert_element_type.38
  2.9 0.0 copy-done
  2.9 0.7 bitcast_multiply_fusion.2.a_ref
  3.6 0.0 copy-start.1
  3.6 0.0 copy-start.3
  3.6 68.6 %shard_map.64 = bf16[512,768]{1,0:T(8,128)(2,1)} custom-call(bf16[512,128]{1,0:T(8,128)(2,1)} %bitcast_multiply_fusion.2.a_ref, bf16[256,768]{1,0:T(8,128)(2,1)} %bitcast_multiply_fusion.1.b_ref), custom_call_target="tpu_custom_call" | custom-call | tf_op jit(solution)/shard_map/pallas_call | solution.py:288
  72.2 0.0 copy-done.1
  72.2 0.0 copy-done.3
  72.2 0.2 convolution_convert_fusion
  72.4 0.1 broadcast_in_dim.16
  72.5 0.1 convert_element_type.43
  72.6 2.1 %bitcast_multiply_fusion = bf16[512,768]{1,0:T(8,128)(2,1)} fusion(bf16[512,768]{1,0:T(8,128)(2,1)} %shard_map.64, bf16[8,768]{1,0:T(8,128)(2,1)S(1)} %convert_element_type.43), kind=kLoop, calls=%fused_computation.1 | loop fusion | flops 393216 | bytes 1585152 | tf_op jit(solution)/shard_map/mul | solution.py:283
  (1 shorter events, 0.0 us)
Async XLA Ops:
  0.9 1.8 %copy-start.2 = (s32[8,2]{0,1:T(2,128)S(1)}, s32[8,2]{0,1:T(2,128)}, u32[]{:S(2)}) copy-start(s32[8,2]{0,1:T(2,128)} %param.8) | copy-start | bytes 196
  0.9 2.1 %copy-start = (bf16[512,128]{1,0:T(8,128)(2,1)S(1)}, bf16[512,128]{1,0:T(8,128)(2,1)}, u32[]{:S(2)}) copy-start(bf16[512,128]{1,0:T(8,128)(2,1)} %param.7) | copy-start | bytes 393220
  3.6 68.6 %copy-start.1 = (s32[128,12]{0,1:T(8,128)S(1)}, s32[128,12]{0,1:T(8,128)}, u32[]{:S(2)}) copy-start(s32[128,12]{0,1:T(8,128)} %param.11) | copy-start | bytes 18436
  3.6 68.6 %copy-start.3 = (s32[8]{0:T(128)S(1)}, s32[8]{0:T(128)}, u32[]{:S(2)}) copy-start(s32[8]{0:T(128)} %param.6) | copy-start | bytes 100

commit v3 on v2

--- a/solution.py
+++ b/solution.py
@@ -11,7 +11,7 @@
 MESH = pl.DeviceIdType.MESH
 
 
-def kernel(a_ref, b_ref, out_ref, a_all, b_all, acc, a_recv, b_recv, e_recv, u_recv, core_send, z_send,
+def kernel(a_hbm, b_hbm, a_mask, b_mask, row_ids, c_keep, out_ref, a_raw, b_raw, a_all, b_all, acc, a_recv, b_recv, e_recv, u_recv, core_send, z_send,
            h_send, y_send, x_send, f_send, e_send, ef_send, u_send, local_sem):
     row = lax.axis_index("row")
     col = lax.axis_index("col")
@@ -31,11 +31,32 @@
     to_core = (row, col_at(h, z, 1 - core))
     to_h = (row, col_at(1 - h, z, core))
 
+    a_fetch = pltpu.make_async_copy(a_hbm, a_raw, local_sem.at[0])
+    b_fetch = pltpu.make_async_copy(b_hbm, b_raw, local_sem.at[1])
+    b_fetch.start()
+    a_fetch.start()
     barrier = pltpu.get_barrier_semaphore()
     partners = (*to_x, *to_y, *to_z, to_core, to_h)
     for partner in partners:
         pl.semaphore_signal(barrier, inc=1, device_id=partner, device_id_type=MESH)
+
+    left = lax.broadcasted_iota(jnp.int32, (TILE, 2 * TILE), 1) < TILE
+
+    def two_blocks(first, second):
+        factor = jnp.where(left, first, second)
+        return factor.astype(jnp.float32)
+
+    b_fetch.wait()
+    for i in range(4):
+        for j in range(6):
+            rows, cols = pl.ds(i * TILE, TILE), pl.ds(j * 2 * TILE, 2 * TILE)
+            b_all[x, y, rows, cols] = b_raw[rows, cols] * two_blocks(b_mask[i, 2 * j], b_mask[i, 2 * j + 1]).astype(jnp.bfloat16)
+    a_fetch.wait()
+    for i in range(8):
+        rows = pl.ds(i * TILE, TILE)
+        a_all[col, rows] = a_raw[rows] * two_blocks(a_mask[0, i], a_mask[1, i]).astype(jnp.bfloat16)
     pl.semaphore_wait(barrier, len(partners))
+    acc[...] = jnp.zeros_like(acc)
 
     def send(source, target, send_sem, recv_sem, to):
         return pltpu.make_async_remote_copy(
@@ -70,10 +91,10 @@
         arrived(edge(xi, y, p), e_recv.at[xi, p])
 
     def own_main(p):
-        return b_ref.at[pl.ds(p * MAIN, MAIN)]
+        return main(x, y, p)
 
     def own_edge(p):
-        return b_ref.at[pl.ds(2 * MAIN + p * EDGE, EDGE)]
+        return edge(x, y, p)
 
     def y_copy(source, yi, p, way):
         return main_copy(source, x, yi, p, y_send.at[way, yi, p], to_y[way])
@@ -102,6 +123,7 @@
     def further(way):
         return (y < NY - 1) if way == 0 else (y > 0)
 
+    a_own = a_all.at[col]
     for p in (0, 1):
         e_copy(p, 0).start()
         e_copy(1 - p, 1).start()
@@ -113,15 +135,10 @@
 
         x_copy(own_main(p), y, p, 0).start()
         x_copy(own_main(1 - p), y, 1 - p, 1).start()
-    z_copy(a_ref, col, 0, 0, 0).start()
-    z_copy(a_ref, col, 0, 1, 0).start()
-    a_copy(a_ref, col, h_send, to_h).start()
-    core_copy(a_ref, col, z, 0).start()
-    local = pltpu.make_async_copy(b_ref, b_all.at[x, y], local_sem)
-    local.start()
-
-    a_all[col] = a_ref[...]
-    acc[...] = jnp.zeros_like(acc)
+    z_copy(a_own, col, 0, 0, 0).start()
+    z_copy(a_own, col, 0, 1, 0).start()
+    a_copy(a_own, col, h_send, to_h).start()
+    core_copy(a_own, col, z, 0).start()
 
     def a_step(kind, step):
         half = h if kind == 0 else 1 - h
@@ -176,7 +193,6 @@
         e_forward(1).start()
 
     def own_bundle():
-        local.wait()
         edge_arrived(x_prev, 1)
         edge_arrived(x_next, 0)
         edge_arrived(x_far, 0)
@@ -245,21 +261,28 @@
     for half in range(NH):
         for zi in range(NZ):
             a_arrived(col_at(half, zi, 1 - core))
+    x_forward(3)
+    u_step(3)
     multiply(0)
     multiply(1)
-    x_forward(3)
     multiply(2)
-    u_step(3)
     multiply(3)
-    out_ref[...] = acc[...].astype(out_ref.dtype)
-
-    a_copy(a_ref, col, h_send, to_h).wait_send()
+    for i in range(8):
+        slot = row_ids[i]
+        held = jnp.maximum(slot, 0)
+        live = jnp.where(slot >= 0, 1, 0)
+        for j in range(6):
+            rows, cols = pl.ds(i * TILE, TILE), pl.ds(j * 2 * TILE, 2 * TILE)
+            keep = jnp.where(left, c_keep[2 * j, held] * live, c_keep[2 * j + 1, held] * live)
+            out_ref[rows, cols] = (acc[rows, cols] * keep.astype(jnp.float32)).astype(out_ref.dtype)
+
+    a_copy(a_own, col, h_send, to_h).wait_send()
     for kind in (0, 1):
         for way in (0, 1):
             for hop in range(a_hops[kind][way]):
-                z_copy(a_ref, col, kind, way, hop).wait_send()
+                z_copy(a_own, col, kind, way, hop).wait_send()
         for zi in range(NZ):
-            core_copy(a_ref, col, zi, kind).wait_send()
+            core_copy(a_own, col, zi, kind).wait_send()
     for way in (0, 1):
         for p in (0, 1):
             e_copy(p, way).wait_send()
@@ -277,20 +300,15 @@
 
 
 def per_device(row_ids, a_tiles, a_mask, b_tiles, b_mask, c_keep):
-    def by_blocks(array, blocks):
-        wide = jnp.repeat(blocks, TILE, axis=1).astype(array.dtype)
-        tall = array.reshape(blocks.shape[0], TILE, array.shape[1])
-        return (tall * wide[:, None, :]).reshape(array.shape)
-
-    a_eff = by_blocks(a_tiles, a_mask)
-    b_eff = by_blocks(b_tiles, b_mask)
     dma = pltpu.SemaphoreType.DMA
     product = pl.pallas_call(
         kernel,
         out_shape=jax.ShapeDtypeStruct((512, 768), jnp.bfloat16),
-        in_specs=[pl.BlockSpec(memory_space=pltpu.VMEM)] * 2,
+        in_specs=[pl.BlockSpec(memory_space=pl.ANY)] * 2 + [pl.BlockSpec(memory_space=pltpu.SMEM)] * 4,
         out_specs=pl.BlockSpec(memory_space=pltpu.VMEM),
         scratch_shapes=[
+            pltpu.VMEM((512, 128), jnp.bfloat16),
+            pltpu.VMEM((256, 768), jnp.bfloat16),
             pltpu.VMEM((32, 512, 128), jnp.bfloat16),
             pltpu.VMEM((NX, NY, 256, 768), jnp.bfloat16),
             pltpu.VMEM((512, 768), jnp.float32),
@@ -307,15 +325,11 @@
             dma((2, 2)),
             dma((2,)),
             dma((2, NY)),
-            dma,
+            dma((2,)),
         ],
         compiler_params=pltpu.CompilerParams(collective_id=0, has_side_effects=True),
-    )(a_eff, b_eff)
-    onehot = (row_ids[:, None] == jnp.arange(c_keep.shape[0], dtype=jnp.int32)[None, :]).astype(
-        jnp.float32
-    )
-    keep = jnp.dot(onehot, c_keep.astype(jnp.float32))
-    return by_blocks(product, keep)
+    )(a_tiles, b_tiles, a_mask.T, b_mask, row_ids, c_keep.T)
+    return product
 
 
 def solution(mesh):

time: 74.9 us -> 68.1 us (0.909)
  other arithmetic: 5.23 us -> 0 us
  Pallas kernels: 68.6 us -> 65.8 us
  local copies, waits for them, and re-layouts: 0.62 us -> 2.06 us
    mul x3 -> x0, other arithmetic: 4.54 us -> none  [by_blocks(): return (tall * wide[:, None, :]).reshape(array.shape)]
    pallas_call x1, Pallas kernels: 68.6 us -> 65.8 us  [per_device(): pl.pallas_call(kernel, out_shape=jax.ShapeDtypeStruct((512, 768), jnp.bfl...]
    unnamed x8 -> x1, local copies, waits for them, and re-layouts: 0.01 us -> 2.06 us
where the time goes in v3:
time: 68.1 us; the launch traced here: 67.8 us
  Pallas kernels  65.8 us (97%)
  local copies, waits for them, and re-layouts  2.06 us (3%)
    pallas_call x1, Pallas kernels, per_device(): pl.pallas_call(kernel, out_shape=jax.ShapeDtypeStruct((512, 768), jnp.bfl...  65.8 us
    unnamed x1, local copies, waits for them, and re-layouts  2.06 us

profile of v3, /device:TPU:1, one launch (start us, length us, event | category | flops | bytes accessed | tf_op | source)
XLA Modules:
  0.0 67.8 jit_solution(6264697951201988901)
XLA Ops:
  0.0 65.8 %shard_map.64 = bf16[512,768]{1,0:T(8,128)(2,1)} custom-call(bf16[512,128]{1,0:T(8,128)(2,1)} %a_hbm.1, bf16[256,768]{1,0:T(8,128)(2,1)} %b_hbm.1, s32[2,8]{1,0:T(2,128)} %bitcast.3, s32[4,12]{1,0:T(4,128)} %b_mask.1, s32[8]{0:T(128)} %row_ids.1, s32[12,128]{1,0:T(8,128)} %bitcast.2), custom_call_target="tpu_custom_call" | custom-call | tf_op jit(solution)/shard_map/pallas_call | solution.py:304
  65.8 2.1 %copy.8 = bf16[512,768]{1,0:T(8,128)(2,1)} copy(bf16[512,768]{1,0:T(8,128)(2,1)} %shard_map.64) | data formatting | bytes 1572864

commit v4 on v3

--- a/solution.py
+++ b/solution.py
@@ -7,12 +7,13 @@
 
 TILE = 64
 NX, NY, NH, NZ = 4, 4, 2, 8
-MAIN, EDGE = 112, 16
+MAIN, EDGE = ((0, 112), (112, 96)), ((208, 16), (224, 32))
+BUNDLE = (208, 48)
 MESH = pl.DeviceIdType.MESH
 
 
-def kernel(a_hbm, b_hbm, a_mask, b_mask, row_ids, c_keep, out_ref, a_raw, b_raw, a_all, b_all, acc, a_recv, b_recv, e_recv, u_recv, core_send, z_send,
-           h_send, y_send, x_send, f_send, e_send, ef_send, u_send, local_sem):
+def kernel(a_hbm, b_hbm, am_hbm, bm_hbm, ids_hbm, keep_hbm, out_ref, a_raw, b_raw, a_mask, b_mask, row_ids, c_keep, a_all, b_all, acc, a_recv, b_recv, e_recv, u_recv, core_send, z_send,
+           h_send, y_send, x_send, f_send, e_send, ef_send, u_send, local_sem, transit, t_send, t_recv):
     row = lax.axis_index("row")
     col = lax.axis_index("col")
     x, y = row // NY, row % NY
@@ -29,14 +30,24 @@
     to_y = ((row_at(x, (y + 1) % NY), col), (row_at(x, (y + NY - 1) % NY), col))
     to_z = ((row, col_at(h, (z + 1) % NZ, core)), (row, col_at(h, (z + NZ - 1) % NZ, core)))
     to_core = (row, col_at(h, z, 1 - core))
-    to_h = (row, col_at(1 - h, z, core))
+
+    ring = 2 * NY
+    place, turn = h * NY + y + ring, 1 - 2 * core
+
+    def ring_at(at):
+        return (row_at(x, at % NY), col_at((at % ring) // NY, z, core))
+
 
     a_fetch = pltpu.make_async_copy(a_hbm, a_raw, local_sem.at[0])
     b_fetch = pltpu.make_async_copy(b_hbm, b_raw, local_sem.at[1])
-    b_fetch.start()
-    a_fetch.start()
+    am_fetch = pltpu.make_async_copy(am_hbm, a_mask, local_sem.at[2])
+    bm_fetch = pltpu.make_async_copy(bm_hbm, b_mask, local_sem.at[3])
+    ids_fetch = pltpu.make_async_copy(ids_hbm, row_ids, local_sem.at[4])
+    keep_fetch = pltpu.make_async_copy(keep_hbm, c_keep, local_sem.at[5])
+    for fetch in (bm_fetch, b_fetch, am_fetch, a_fetch, ids_fetch, keep_fetch):
+        fetch.start()
     barrier = pltpu.get_barrier_semaphore()
-    partners = (*to_x, *to_y, *to_z, to_core, to_h)
+    partners = (*to_x, *to_z, to_core, *(ring_at(place + hops) for hops in (1, -1, 3, -3)))
     for partner in partners:
         pl.semaphore_signal(barrier, inc=1, device_id=partner, device_id_type=MESH)
 
@@ -46,11 +57,13 @@
         factor = jnp.where(left, first, second)
         return factor.astype(jnp.float32)
 
+    bm_fetch.wait()
     b_fetch.wait()
     for i in range(4):
         for j in range(6):
             rows, cols = pl.ds(i * TILE, TILE), pl.ds(j * 2 * TILE, 2 * TILE)
             b_all[x, y, rows, cols] = b_raw[rows, cols] * two_blocks(b_mask[i, 2 * j], b_mask[i, 2 * j + 1]).astype(jnp.bfloat16)
+    am_fetch.wait()
     a_fetch.wait()
     for i in range(8):
         rows = pl.ds(i * TILE, TILE)
@@ -73,13 +86,13 @@
         arrived(a_all.at[q], a_recv.at[q])
 
     def main(xi, yi, p):
-        return b_all.at[xi, yi, pl.ds(p * MAIN, MAIN)]
+        return b_all.at[xi, yi, pl.ds(*MAIN[p])]
 
     def edge(xi, yi, p):
-        return b_all.at[xi, yi, pl.ds(2 * MAIN + p * EDGE, EDGE)]
+        return b_all.at[xi, yi, pl.ds(*EDGE[p])]
 
     def bundle(yi):
-        return b_all.at[:, yi, pl.ds(2 * MAIN, 2 * EDGE)]
+        return b_all.at[:, yi, pl.ds(*BUNDLE)]
 
     def main_copy(source, xi, yi, p, send_sem, to):
         return send(source, main(xi, yi, p), send_sem, b_recv.at[xi, yi, p], to)
@@ -137,7 +150,7 @@
         x_copy(own_main(1 - p), y, 1 - p, 1).start()
     z_copy(a_own, col, 0, 0, 0).start()
     z_copy(a_own, col, 0, 1, 0).start()
-    a_copy(a_own, col, h_send, to_h).start()
+    send(a_own, transit, h_send, t_recv, ring_at(place + turn)).start()
     core_copy(a_own, col, z, 0).start()
 
     def a_step(kind, step):
@@ -151,6 +164,10 @@
                     z_copy(a_all.at[q], q, kind, way, step).start()
                 core_copy(a_all.at[q], q, zi, kind).start()
 
+    def relay():
+        q = col_at(((place - turn) % ring) // NY, z, core)
+        return a_copy(transit, q, t_send, ring_at(place + 3 * turn))
+
     def a_other_half():
         q = col_at(1 - h, z, core)
         a_arrived(q)
@@ -243,6 +260,8 @@
     a_step(0, 1)
     x_forward(0)
     y_step(1)
+    arrived(transit, t_recv)
+    relay().start()
     own_bundle()
     a_step(0, 2)
     x_forward(1)
@@ -267,6 +286,8 @@
     multiply(1)
     multiply(2)
     multiply(3)
+    ids_fetch.wait()
+    keep_fetch.wait()
     for i in range(8):
         slot = row_ids[i]
         held = jnp.maximum(slot, 0)
@@ -276,7 +297,8 @@
             keep = jnp.where(left, c_keep[2 * j, held] * live, c_keep[2 * j + 1, held] * live)
             out_ref[rows, cols] = (acc[rows, cols] * keep.astype(jnp.float32)).astype(out_ref.dtype)
 
-    a_copy(a_own, col, h_send, to_h).wait_send()
+    send(a_own, transit, h_send, t_recv, ring_at(place + turn)).wait_send()
+    relay().wait_send()
     for kind in (0, 1):
         for way in (0, 1):
             for hop in range(a_hops[kind][way]):
@@ -304,11 +326,15 @@
     product = pl.pallas_call(
         kernel,
         out_shape=jax.ShapeDtypeStruct((512, 768), jnp.bfloat16),
-        in_specs=[pl.BlockSpec(memory_space=pl.ANY)] * 2 + [pl.BlockSpec(memory_space=pltpu.SMEM)] * 4,
+        in_specs=[pl.BlockSpec(memory_space=pltpu.HBM)] * 6,
         out_specs=pl.BlockSpec(memory_space=pltpu.VMEM),
         scratch_shapes=[
             pltpu.VMEM((512, 128), jnp.bfloat16),
             pltpu.VMEM((256, 768), jnp.bfloat16),
+            pltpu.SMEM((2, 8), jnp.int32),
+            pltpu.SMEM((4, 12), jnp.int32),
+            pltpu.SMEM((8,), jnp.int32),
+            pltpu.SMEM((12, 128), jnp.int32),
             pltpu.VMEM((32, 512, 128), jnp.bfloat16),
             pltpu.VMEM((NX, NY, 256, 768), jnp.bfloat16),
             pltpu.VMEM((512, 768), jnp.float32),
@@ -325,7 +351,10 @@
             dma((2, 2)),
             dma((2,)),
             dma((2, NY)),
-            dma((2,)),
+            dma((6,)),
+            pltpu.VMEM((512, 128), jnp.bfloat16),
+            dma,
+            dma,
         ],
         compiler_params=pltpu.CompilerParams(collective_id=0, has_side_effects=True),
     )(a_tiles, b_tiles, a_mask.T, b_mask, row_ids, c_keep.T)

time: 68.1 us -> 69 us (1.013)
  Pallas kernels: 65.8 us -> 66.8 us
    pallas_call x1, Pallas kernels: 65.8 us -> 66.8 us  [per_device(): pl.pallas_call(kernel, out_shape=jax.ShapeDtypeStruct((512, 768), jnp.bfl...]
where the time goes in v4:
time: 69 us; the launch traced here: 68.8 us
  Pallas kernels  66.8 us (97%)
  local copies, waits for them, and re-layouts  2.06 us (3%)
    pallas_call x1, Pallas kernels, per_device(): pl.pallas_call(kernel, out_shape=jax.ShapeDtypeStruct((512, 768), jnp.bfl...  66.8 us
    unnamed x1, local copies, waits for them, and re-layouts  2.06 us

profile of v4, /device:TPU:1, one launch (start us, length us, event | category | flops | bytes accessed | tf_op | source)
XLA Modules:
  0.0 68.8 jit_solution(15529516152617301877)
XLA Ops:
  0.0 66.8 %shard_map.64 = bf16[512,768]{1,0:T(8,128)(2,1)} custom-call(bf16[512,128]{1,0:T(8,128)(2,1)} %a_hbm.1, bf16[256,768]{1,0:T(8,128)(2,1)} %b_hbm.1, s32[2,8]{1,0:T(2,128)} %bitcast.3, s32[4,12]{1,0:T(4,128)} %bm_hbm.1, s32[8]{0:T(128)} %ids_hbm.1, s32[12,128]{1,0:T(8,128)} %bitcast.2), custom_call_target="tpu_custom_call" | custom-call | tf_op jit(solution)/shard_map/pallas_call | solution.py:326
  66.8 2.1 %copy.8 = bf16[512,768]{1,0:T(8,128)(2,1)} copy(bf16[512,768]{1,0:T(8,128)(2,1)} %shard_map.64) | data formatting | bytes 1572864

commit v5 on v3

--- a/solution.py
+++ b/solution.py
@@ -11,7 +11,7 @@
 MESH = pl.DeviceIdType.MESH
 
 
-def kernel(a_hbm, b_hbm, a_mask, b_mask, row_ids, c_keep, out_ref, a_raw, b_raw, a_all, b_all, acc, a_recv, b_recv, e_recv, u_recv, core_send, z_send,
+def kernel(a_hbm, b_hbm, am_hbm, bm_hbm, ids_hbm, keep_hbm, out_ref, a_raw, b_raw, a_mask, b_mask, row_ids, c_keep, a_all, b_all, acc, a_recv, b_recv, e_recv, u_recv, core_send, z_send,
            h_send, y_send, x_send, f_send, e_send, ef_send, u_send, local_sem):
     row = lax.axis_index("row")
     col = lax.axis_index("col")
@@ -33,8 +33,12 @@
 
     a_fetch = pltpu.make_async_copy(a_hbm, a_raw, local_sem.at[0])
     b_fetch = pltpu.make_async_copy(b_hbm, b_raw, local_sem.at[1])
-    b_fetch.start()
-    a_fetch.start()
+    am_fetch = pltpu.make_async_copy(am_hbm, a_mask, local_sem.at[2])
+    bm_fetch = pltpu.make_async_copy(bm_hbm, b_mask, local_sem.at[3])
+    ids_fetch = pltpu.make_async_copy(ids_hbm, row_ids, local_sem.at[4])
+    keep_fetch = pltpu.make_async_copy(keep_hbm, c_keep, local_sem.at[5])
+    for fetch in (bm_fetch, b_fetch, am_fetch, a_fetch, ids_fetch, keep_fetch):
+        fetch.start()
     barrier = pltpu.get_barrier_semaphore()
     partners = (*to_x, *to_y, *to_z, to_core, to_h)
     for partner in partners:
@@ -46,11 +50,13 @@
         factor = jnp.where(left, first, second)
         return factor.astype(jnp.float32)
 
+    bm_fetch.wait()
     b_fetch.wait()
     for i in range(4):
         for j in range(6):
             rows, cols = pl.ds(i * TILE, TILE), pl.ds(j * 2 * TILE, 2 * TILE)
             b_all[x, y, rows, cols] = b_raw[rows, cols] * two_blocks(b_mask[i, 2 * j], b_mask[i, 2 * j + 1]).astype(jnp.bfloat16)
+    am_fetch.wait()
     a_fetch.wait()
     for i in range(8):
         rows = pl.ds(i * TILE, TILE)
@@ -240,12 +246,12 @@
         add_block(x_far, yi)
 
     edges_forward()
+    x_forward(0)
     a_step(0, 1)
-    x_forward(0)
     y_step(1)
     own_bundle()
+    x_forward(1)
     a_step(0, 2)
-    x_forward(1)
     a_other_half()
     y_step(2)
     a_step(0, 3)
@@ -267,6 +273,8 @@
     multiply(1)
     multiply(2)
     multiply(3)
+    ids_fetch.wait()
+    keep_fetch.wait()
     for i in range(8):
         slot = row_ids[i]
         held = jnp.maximum(slot, 0)
@@ -304,11 +312,15 @@
     product = pl.pallas_call(
         kernel,
         out_shape=jax.ShapeDtypeStruct((512, 768), jnp.bfloat16),
-        in_specs=[pl.BlockSpec(memory_space=pl.ANY)] * 2 + [pl.BlockSpec(memory_space=pltpu.SMEM)] * 4,
+        in_specs=[pl.BlockSpec(memory_space=pltpu.HBM)] * 6,
         out_specs=pl.BlockSpec(memory_space=pltpu.VMEM),
         scratch_shapes=[
             pltpu.VMEM((512, 128), jnp.bfloat16),
             pltpu.VMEM((256, 768), jnp.bfloat16),
+            pltpu.SMEM((2, 8), jnp.int32),
+            pltpu.SMEM((4, 12), jnp.int32),
+            pltpu.SMEM((8,), jnp.int32),
+            pltpu.SMEM((12, 128), jnp.int32),
             pltpu.VMEM((32, 512, 128), jnp.bfloat16),
             pltpu.VMEM((NX, NY, 256, 768), jnp.bfloat16),
             pltpu.VMEM((512, 768), jnp.float32),
@@ -325,7 +337,7 @@
             dma((2, 2)),
             dma((2,)),
             dma((2, NY)),
-            dma((2,)),
+            dma((6,)),
         ],
         compiler_params=pltpu.CompilerParams(collective_id=0, has_side_effects=True),
     )(a_tiles, b_tiles, a_mask.T, b_mask, row_ids, c_keep.T)

time: 68.1 us -> 69.9 us (1.026)
  Pallas kernels: 65.8 us -> 67.7 us
    pallas_call x1, Pallas kernels: 65.8 us -> 67.7 us  [per_device(): pl.pallas_call(kernel, out_shape=jax.ShapeDtypeStruct((512, 768), jnp.bfl...]
where the time goes in v5:
time: 69.9 us; the launch traced here: 69.7 us
  Pallas kernels  67.7 us (97%)
  local copies, waits for them, and re-layouts  2.06 us (3%)
    pallas_call x1, Pallas kernels, per_device(): pl.pallas_call(kernel, out_shape=jax.ShapeDtypeStruct((512, 768), jnp.bfl...  67.7 us
    unnamed x1, local copies, waits for them, and re-layouts  2.06 us

profile of v5, /device:TPU:1, one launch (start us, length us, event | category | flops | bytes accessed | tf_op | source)
XLA Modules:
  0.0 69.7 jit_solution(13109010450156860313)
XLA Ops:
  0.0 67.7 %shard_map.64 = bf16[512,768]{1,0:T(8,128)(2,1)} custom-call(bf16[512,128]{1,0:T(8,128)(2,1)} %a_hbm.1, bf16[256,768]{1,0:T(8,128)(2,1)} %b_hbm.1, s32[2,8]{1,0:T(2,128)} %bitcast.3, s32[4,12]{1,0:T(4,128)} %bm_hbm.1, s32[8]{0:T(128)} %ids_hbm.1, s32[12,128]{1,0:T(8,128)} %bitcast.2), custom_call_target="tpu_custom_call" | custom-call | tf_op jit(solution)/shard_map/pallas_call | solution.py:312
  67.7 2.1 %copy.8 = bf16[512,768]{1,0:T(8,128)(2,1)} copy(bf16[512,768]{1,0:T(8,128)(2,1)} %shard_map.64) | data formatting | bytes 1572864
